TPU v7x, 128 devices: a whole 4x4x4 slice. The times are simulated.
128 devices in a mesh: space: 32 (over x, y, core), member: 4 (over z).
Axes of the slice: x: 4, y: 4, z: 4, core: 2. Of those that a mesh axis runs over, the one named last changes fastest.
Arguments:
- latent: bfloat16 [16, 16384, 1024], P('member', 'space'), may hold values from -6 to 6
- w_in: bfloat16 [1024, 1024], replicated, may hold values from -0.1875 to 0.1875
- b_in: float32 [1024], replicated, may hold values from -3 to 3
- w_out: bfloat16 [1024, 96], replicated, may hold values from -0.1875 to 0.1875
- b_out: float32 [96], replicated, may hold values from -3 to 3
- target: float32 [16384, 96], P('space'), may hold values from -6 to 6
- area: float32 [16384], P('space'), may hold values from 0.5 to 40, as said below
- cell_of: int32 [16384], P('space'), may hold values from 0 to 1023, as said below
Outputs:
- latent_grad: bfloat16 [16, 16384, 1024], P('member', 'space')
- scores: float32 [2], replicated
Inputs may be any that keep to these rules, and one draw needn't show every extreme that they name: `cell_of`: every node lies in one coarse cell; some cells hold no node. Positive area of each node.
All inputs are finite; a program needn't handle non-finite values.
Results may differ from a plain program's by a relative error of at most 0.03.
Values may be sent and summed in bfloat16 or wider, within the bound.
No kernel may reach another device: no remote copies, remote signals or barrier semaphores. Data moves between devices by JAX's collectives and lax.ppermute only.
A program may use at most 64 MiB of HBM per device.

v0:
```python
import functools
import math

import jax
import jax.numpy as jnp
from jax import lax
from jax.sharding import Mesh
from jax.sharding import PartitionSpec as P

CELL_DEV = 32
SPACE = ("space_0", "space_1", "space_2")
SPACE_MEMBER = ("space_0", "space_1", "space_2", "member")


epsilon = 1e-05
loss_scale = 4096.0


def joined_along(parts, dim):
    parts = jnp.moveaxis(parts, 0, dim)
    dims = parts.shape
    return parts.reshape(*dims[:dim], dims[dim] * dims[dim + 1], *dims[dim + 2 :])


def from_everyone(shard, axis):
    copies = jnp.broadcast_to(shard, (lax.axis_size(axis), *shard.shape))
    return lax.all_to_all(copies, axis, split_axis=0, concat_axis=0, tiled=True)


def collect(shard, axis, dim):
    return joined_along(from_everyone(shard, axis), dim)


def in_blocks(shard, dim, size):
    dims = shard.shape
    parts = shard.reshape(*dims[:dim], size, dims[dim] // size, *dims[dim + 1 :])
    return jnp.moveaxis(parts, dim, 0)


def sent_and_summed(shard, axis, dim):
    parts = in_blocks(shard, dim, lax.axis_size(axis))
    arrived = lax.all_to_all(parts, axis, split_axis=0, concat_axis=0, tiled=True)
    return arrived.astype(jnp.float32).sum(axis=0)


def sent_together(arrays, axis, dim, along):
    widths = [math.prod(a.shape[along:]) for a in arrays]
    both = jnp.concatenate(
        [a.reshape(*a.shape[:along], w) for a, w in zip(arrays, widths)], axis=along
    )
    whole = sent_and_summed(both, axis, dim)
    parts = jnp.split(whole, [sum(widths[:k]) for k in range(1, len(widths))], axis=along)
    return tuple((b.reshape(*whole.shape[:along], *a.shape[along:]) for a, b in zip(arrays, parts)))


def over_axes(shard, axes):
    return functools.reduce(lax.psum, axes, shard)


def silu_slope(preact):
    sigma = jax.nn.sigmoid(preact)
    return sigma * (1.0 + preact * (1.0 - sigma))


def energy(own_part, everyone, truths, weight, own_ids):
    members = everyone.shape[0]
    variables = everyone.shape[1]
    to_truth = own_part - truths[None]
    truth_dist = jnp.sqrt(jnp.mean(to_truth * to_truth, axis=1) + epsilon)
    between = own_part[:, None] - everyone[None]
    pair_dist = jnp.sqrt(jnp.mean(between * between, axis=2) + epsilon)
    distinct = (own_ids[:, None] != jnp.arange(members, dtype=jnp.int32)[None]).astype(
        own_part.dtype
    )
    pair_weight = distinct[:, :, None] / pair_dist
    node_loss = weight * (
        jnp.sum(truth_dist, axis=0) / members
        - jnp.sum(distinct[:, :, None] * pair_dist, axis=(0, 1)) / (2.0 * members * (members - 1))
    )
    gradient = weight * (
        to_truth / truth_dist[:, None] / (members * variables)
        - jnp.sum(between * pair_weight[:, :, None], axis=1) / (members * (members - 1) * variables)
    )
    return (node_loss, gradient)


def unpack(table, members, variables):
    return table.astype(jnp.float32).reshape(table.shape[0], members, variables).transpose(1, 2, 0)


def pack(gradient):
    members, variables, columns = gradient.shape
    return gradient.astype(jnp.bfloat16).transpose(2, 0, 1).reshape(columns, members * variables)


def shards(latent, w_in, b_in, w_out, b_out, target, area, cell_of):
    member_local, node_count, latent_width = latent.shape
    variables = w_out.shape[1]
    flat_rows = latent.reshape(member_local * node_count, latent_width)
    preact = jnp.dot(flat_rows, w_in, preferred_element_type=jnp.float32) + b_in
    activation = jax.nn.silu(preact).astype(jnp.bfloat16)
    predictions = (jnp.dot(activation, w_out, preferred_element_type=jnp.float32) + b_out).astype(
        jnp.bfloat16
    )
    flattened = (
        predictions.reshape(member_local, node_count, variables)
        .transpose(1, 0, 2)
        .reshape(node_count, member_local * variables)
    )
    member_axis = lax.axis_size("member")
    member_place = lax.axis_index("member")
    space_axis = lax.axis_size(SPACE)
    members = member_local * member_axis
    own_ids = member_place * member_local + jnp.arange(member_local, dtype=jnp.int32)
    gathered = collect(flattened, "member", 1)
    everyone = unpack(gathered, members, variables)
    own_part = lax.dynamic_slice_in_dim(everyone, member_place * member_local, member_local, 0)
    fine_loss, fine_grad = energy(own_part, everyone, target.T, area, own_ids)
    fine_part = lax.optimization_barrier(pack(fine_grad))
    cells = CELL_DEV * space_axis
    onehot = jnp.arange(cells, dtype=jnp.int32)[:, None] == cell_of[None, :]
    picker = onehot.astype(jnp.bfloat16)
    cell_sum = jnp.dot(picker, flattened, preferred_element_type=jnp.float32)
    counts = jnp.sum(onehot.astype(jnp.float32), axis=1)
    cell_area = jnp.sum(jnp.where(onehot, area[None, :], 0.0), axis=1)
    target_sum = jnp.dot(onehot.astype(jnp.float32), target)
    owned_sum, owned_counts, owned_area, owned_target = sent_together(
        (
            cell_sum.astype(jnp.bfloat16),
            counts.astype(jnp.bfloat16),
            cell_area.astype(jnp.bfloat16),
            target_sum.astype(jnp.bfloat16),
        ),
        SPACE,
        0,
        1,
    )
    divisor = jnp.maximum(owned_counts, 1.0)
    cell_mean = (owned_sum / divisor[:, None]).astype(jnp.bfloat16)
    all_means = unpack(collect(cell_mean, "member", 1), members, variables)
    own_means = lax.dynamic_slice_in_dim(all_means, member_place * member_local, member_local, 0)
    cell_target = (owned_target / divisor[:, None]).T
    coarse_loss, coarse_grad = energy(own_means, all_means, cell_target, owned_area, own_ids)
    coarse_total = jnp.sum(coarse_loss)
    every_piece = collect(pack(coarse_grad / divisor[None, None, :]), SPACE, 0)
    coarse_part = lax.dot_general(
        picker, every_piece, (((0,), (0,)), ((), ())), preferred_element_type=jnp.float32
    )
    upstream = (fine_part.astype(jnp.float32) + coarse_part).astype(jnp.bfloat16)
    upstream_rows = (
        upstream.reshape(node_count, member_local, variables)
        .transpose(1, 0, 2)
        .reshape(member_local * node_count, variables)
    )
    hidden_grad = lax.dot_general(
        upstream_rows, w_out, (((1,), (1,)), ((), ())), preferred_element_type=jnp.float32
    )
    preact_grad = (hidden_grad * silu_slope(preact)).astype(jnp.bfloat16)
    latent_raw = lax.dot_general(
        preact_grad, w_in, (((1,), (1,)), ((), ())), preferred_element_type=jnp.float32
    )
    fine_total = jnp.sum(fine_loss)
    fine_total, coarse_total, total_area = (
        over_axes(fine_total, SPACE_MEMBER),
        over_axes(coarse_total, SPACE_MEMBER),
        over_axes(jnp.sum(area) / member_axis, SPACE_MEMBER),
    )
    factor = loss_scale * (node_count * space_axis) / total_area
    latent_grad = (
        (latent_raw * factor).astype(jnp.bfloat16).reshape(member_local, node_count, latent_width)
    )
    scores = jnp.stack([fine_total, coarse_total]) / total_area
    return (latent_grad, scores)


def solution(mesh):
    split = Mesh(
        mesh.devices.reshape(4, 4, 2, mesh.shape["member"]),
        ("space_0", "space_1", "space_2", "member"),
    )
    return jax.shard_map(
        shards,
        mesh=split,
        in_specs=(P("member", SPACE, None), P(), P(), P(), P(), P(SPACE, None), P(SPACE), P(SPACE)),
        out_specs=(P("member", SPACE, None), P()),
        check_vma=False,
    )
```

profile of v0, /device:TPU:0, one launch (start us, length us, event | category | flops | bytes accessed | tf_op | source)
XLA Modules:
  0.0 146.7 jit_solution(12810374830716297491)
XLA Ops:
  0.6 1.5 %convert_reduce_fusion.1 = (bf16[1024]{0:T(1024)(128)(2,1)S(1)}, bf16[1024]{0:T(1024)(128)(2,1)S(1)}) fusion(s32[512]{0:T(512)} %param.15, f32[512]{0:T(512)} %param.14), kind=kLoop, calls=%fused_computation.13 | loop fusion | flops 2619392 | bytes 8192 | tf_op jit(solution)/shard_map/reduce_sum | solution.py:124
  2.1 1.5 fusion.11
  4.7 6.3 %fusion.31 = f32[2048,1024]{1,0:T(8,128)S(1)} fusion(bf16[2048,1024]{1,0:T(8,128)(2,1)} %bitcast.84, bf16[1024,1024]{1,0:T(8,128)(2,1)S(1)} %copy-done), kind=kOutput, calls=%fused_computation.70 | convolution fusion | flops 4294967296 | bytes 14680064 | tf_op jit(solution)/shard_map/dot_general | solution.py:100
  11.1 2.7 %fusion.4 = bf16[2048,96]{0,1:T(8,128)(2,1)S(1)} fusion(bf16[1024,96]{0,1:T(8,128)(2,1)S(1)} %copy-done.5, f32[2048,1024]{1,0:T(8,128)S(1)} %fusion.31, f32[1024]{0:T(1024)S(1)} %copy-done.7, f32[96]{0:T(128)S(1)} %copy-done.9), kind=kOutput, calls=%fused_computation.10 | convolution fusion | flops 415629312 | bytes 8982912 | tf_op jit(solution)/shard_map/dot_general | solution.py:102
  13.8 0.5 copy-done.10
  14.3 0.7 fusion.8
  15.1 1.3 pad_maximum_fusion
  16.3 7.4 %all-to-all-start.1 = ((bf16[32,32,482]{2,1,0:T(8,128)(2,1)}), bf16[32,32,482]{2,1,0:T(8,128)(2,1)S(1)}, u32[]{:S(2)}, u32[]{:S(2)}) async-start(bf16[32,32,482]{2,1,0:T(8,128)(2,1)} %pad_maximum_fusion), calls=%async_computation.1 | async-start | bytes 2097152 | tf_op jit(solution)/shard_map/all_to_all | solution.py:42
  23.9 16.7 %all-to-all-done.1 = bf16[32,32,482]{2,1,0:T(8,128)(2,1)S(1)} async-done(((bf16[32,32,482]{2,1,0:T(8,128)(2,1)}), bf16[32,32,482]{2,1,0:T(8,128)(2,1)S(1)}, u32[]{:S(2)}, u32[]{:S(2)}) %all-to-all-start.1) | async-done | bytes 987168 | tf_op jit(solution)/shard_map/all_to_all | solution.py:42
  41.5 0.7 broadcast_in_dim.17
  42.1 5.3 %all-to-all-start.2 = ((bf16[4,32,384]{2,1,0:T(8,128)(2,1)}), bf16[4,32,384]{2,1,0:T(8,128)(2,1)S(1)}, u32[]{:S(2)}, u32[]{:S(2)}) async-start(bf16[4,32,384]{2,1,0:T(8,128)(2,1)} %broadcast_in_dim.17), calls=%async_computation.2 | async-start | bytes 196608 | tf_op jit(solution)/shard_map/all_to_all | solution.py:27
  47.4 0.8 slice_divide_fusion.1
  48.2 5.0 %all-to-all-done.2 = bf16[4,32,384]{2,1,0:T(8,128)(2,1)S(1)} async-done(((bf16[4,32,384]{2,1,0:T(8,128)(2,1)}), bf16[4,32,384]{2,1,0:T(8,128)(2,1)S(1)}, u32[]{:S(2)}, u32[]{:S(2)}) %all-to-all-start.2) | async-done | bytes 98336 | tf_op jit(solution)/shard_map/all_to_all | solution.py:27
  53.2 1.3 broadcast_in_dim.14
  54.5 4.4 %all-to-all-start = ((bf16[4,512,384]{1,2,0:T(8,128)(2,1)}), bf16[4,512,384]{1,2,0:T(8,128)(2,1)}, u32[]{:S(2)}, u32[]{:S(2)}) async-start(bf16[4,512,384]{1,2,0:T(8,128)(2,1)} %broadcast_in_dim.14), calls=%async_computation | async-start | bytes 3145728 | tf_op jit(solution)/shard_map/all_to_all | solution.py:27
  60.5 0.6 multiply_reduce_fusion.5
  61.2 17.9 %all-to-all-done = bf16[4,512,384]{1,2,0:T(8,128)(2,1)} async-done(((bf16[4,512,384]{1,2,0:T(8,128)(2,1)}), bf16[4,512,384]{1,2,0:T(8,128)(2,1)}, u32[]{:S(2)}, u32[]{:S(2)}) %all-to-all-start) | async-done | bytes 1572896 | tf_op jit(solution)/shard_map/all_to_all | solution.py:27
  79.1 1.0 broadcast_in_dim.18
  80.0 4.6 %all-to-all-start.3 = ((bf16[32,32,384]{2,1,0:T(8,128)(2,1)}), bf16[32,32,384]{2,1,0:T(8,128)(2,1)}, u32[]{:S(2)}, u32[]{:S(2)}) async-start(bf16[32,32,384]{2,1,0:T(8,128)(2,1)} %broadcast_in_dim.18), calls=%async_computation.3 | async-start | bytes 1572864 | tf_op jit(solution)/shard_map/all_to_all | solution.py:27
  84.7 1.8 %convert_element_type.125 = f32[4,512,384]{1,2,0:T(8,128)S(1)} convert(bf16[4,512,384]{1,2,0:T(8,128)(2,1)} %all-to-all-done) | non-fusion elementwise | flops 786432 | bytes 4718592 | tf_op jit(solution)/shard_map/convert_element_type | solution.py:88
  86.7 1.4 copy-done.1
  88.2 1.6 %fusion = f32[4,16,512]{2,1,0:T(8,128)S(1)} fusion(f32[16,96,512]{2,1,0:T(8,128)S(1)} %bitcast.68, f32[4,96,512]{2,1,0:T(8,128)S(1)} %get-tuple-element.21), kind=kLoop, calls=%fused_computation.2 | loop fusion | flops 9404416 | bytes 4063232 | tf_op jit(solution)/shard_map/reduce_sum | solution.py:71
  89.9 0.6 multiply_reduce_fusion.4
  91.1 11.4 %all-reduce.2 = (f32[]{:T(128)}, f32[]{:T(128)}, f32[]{:T(128)}) all-reduce(f32[]{:T(128)S(6)} %div.190, f32[]{:T(128)} %multiply_reduce_fusion.5, f32[]{:T(128)} %get-tuple-element.4), channel_id=1, replica_groups=mesh['space_0'=4,'space_1'=4,'space_2'=2,'member'=4] {'space_0'}, use_global_device_ids=true, to_apply=%region_10.11 | all-reduce | flops 3 | bytes 24 | tf_op jit(solution)/shard_map/psum | solution.py:57
  102.5 11.1 %all-reduce.1 = (f32[]{:T(128)}, f32[]{:T(128)}, f32[]{:T(128)}) all-reduce(f32[]{:T(128)} %get-tuple-element.14, f32[]{:T(128)} %get-tuple-element.15, f32[]{:T(128)} %get-tuple-element.16), channel_id=1, replica_groups=mesh['space_0'=4,'space_1'=4,'space_2'=2,'member'=4] {'space_1'}, use_global_device_ids=true, to_apply=%region_11.12 | all-reduce | flops 3 | bytes 24 | tf_op jit(solution)/shard_map/psum | solution.py:57
  113.6 3.1 %all-reduce.3 = (f32[]{:T(128)}, f32[]{:T(128)}, f32[]{:T(128)}) all-reduce(f32[]{:T(128)} %get-tuple-element.11, f32[]{:T(128)} %get-tuple-element.12, f32[]{:T(128)} %get-tuple-element.13), channel_id=1, replica_groups=mesh['space_0'=4,'space_1'=4,'space_2'=2,'member'=4] {'space_2'}, use_global_device_ids=true, to_apply=%region_12.13 | all-reduce | flops 3 | bytes 24 | tf_op jit(solution)/shard_map/psum | solution.py:57
  116.7 9.7 %all-reduce = (f32[]{:T(128)}, f32[1]{0:T(128)}, f32[1]{0:T(128)}) all-reduce(f32[]{:T(128)} %get-tuple-element.17, f32[1]{0:T(128)} %bitcast.26, f32[1]{0:T(128)} %bitcast.25), channel_id=1, replica_groups=mesh['space_0'=4,'space_1'=4,'space_2'=2,'member'=4] {'member'}, use_global_device_ids=true, to_apply=%region_13.14 | all-reduce | flops 3 | bytes 24 | tf_op jit(solution)/shard_map/psum | solution.py:57
  126.4 3.4 %fusion.1 = f32[4,96,512]{2,1,0:T(8,128)S(1)} fusion(f32[4,16,512]{2,1,0:T(8,128)S(1)} %get-tuple-element.22, f32[16,96,512]{2,1,0:T(8,128)} %bitcast.69, f32[4,96,512]{2,1,0:T(8,128)S(1)} %get-tuple-element.21), kind=kLoop, calls=%fused_computation.3 | loop fusion | flops 9240576 | bytes 4849664 | tf_op jit(solution)/shard_map/reduce_sum | solution.py:82
  129.8 1.4 fusion.18
  131.8 2.3 %maximum_divide_fusion = f32[2]{0:T(128)} fusion(f32[1]{0:T(128)} %get-tuple-element.9, f32[1]{0:T(128)} %get-tuple-element.10, f32[]{:T(128)} %get-tuple-element.8), kind=kLoop, calls=%fused_computation.64 | loop fusion | flops 4 | bytes 20 | tf_op jit(solution)/shard_map/div | solution.py:172
  134.1 1.8 %fusion.10 = bf16[512,384]{0,1:T(8,128)(2,1)S(1)} fusion(bf16[1024,384]{1,0:T(8,128)(2,1)} %bitcast.21, s32[512]{0:T(512)S(1)} %copy-done.8, bf16[512,384]{0,1:T(8,128)(2,1)S(1)} %bitcast.83), kind=kOutput, calls=%fused_computation.22 | convolution fusion | flops 403767296 | bytes 1574912 | tf_op jit(solution)/shard_map/dot_general | solution.py:146
  136.3 10.3 %multiply_convert_fusion = bf16[2048,1024]{1,0:T(8,128)(2,1)} fusion(bf16[1024,1024]{1,0:T(8,128)(2,1)S(1)} %copy-done, f32[]{:T(128)S(6)} %div.191, f32[2048,1024]{1,0:T(8,128)} %copy-done.10, bf16[2048,96]{0,1:T(8,128)(2,1)S(1)} %bitcast.80, bf16[1024,96]{0,1:T(8,128)(2,1)S(1)} %copy-done.6, f32[1024]{0:T(1024)S(1)} %copy-done.7), kind=kOutput, calls=%fused_computation.4 | convolution fusion | flops 4722786304 | bytes 15273988 | tf_op jit(solution)/shard_map/dot_general | solution.py:159
  (50 shorter events, 4.3 us)
Async XLA Ops:
  0.6 4.0 %copy-start = (bf16[1024,1024]{1,0:T(8,128)(2,1)S(1)}, bf16[1024,1024]{1,0:T(8,128)(2,1)}, u32[]{:S(2)}) copy-start(bf16[1024,1024]{1,0:T(8,128)(2,1)} %param.9) | copy-start | bytes 6291460
  4.7 6.4 %copy-start.5 = (bf16[1024,96]{0,1:T(8,128)(2,1)S(1)}, bf16[1024,96]{0,1:T(8,128)(2,1)}, u32[]{:S(2)}) copy-start(bf16[1024,96]{0,1:T(8,128)(2,1)} %param.11) | copy-start | bytes 589828
  4.7 6.4 %copy-start.7 = (f32[1024]{0:T(1024)S(1)}, f32[1024]{0:T(1024)}, u32[]{:S(2)}) copy-start(f32[1024]{0:T(1024)} %param.10) | copy-start | bytes 12292
  4.7 6.4 %copy-start.9 = (f32[96]{0:T(128)S(1)}, f32[96]{0:T(128)}, u32[]{:S(2)}) copy-start(f32[96]{0:T(128)} %param.12) | copy-start | bytes 1156
  11.1 3.2 %copy-start.10 = (f32[2048,1024]{1,0:T(8,128)}, f32[2048,1024]{1,0:T(8,128)S(1)}, u32[]{:S(2)}) copy-start(f32[2048,1024]{1,0:T(8,128)S(1)} %fusion.31) | copy-start | bytes 25165828
  11.1 3.2 %copy-start.8 = (s32[512]{0:T(512)S(1)}, s32[512]{0:T(512)}, u32[]{:S(2)}) copy-start(s32[512]{0:T(512)} %param.15) | copy-start | bytes 6148
  16.3 24.2 %all-to-all-start.1 = ((bf16[32,32,482]{2,1,0:T(8,128)(2,1)}), bf16[32,32,482]{2,1,0:T(8,128)(2,1)S(1)}, u32[]{:S(2)}, u32[]{:S(2)}) async-start(bf16[32,32,482]{2,1,0:T(8,128)(2,1)} %pad_maximum_fusion), calls=%async_computation.1 | async-start | bytes 2097152 | tf_op jit(solution)/shard_map/all_to_all | solution.py:42
  40.7 0.6 copy-start.3
  42.1 11.1 %all-to-all-start.2 = ((bf16[4,32,384]{2,1,0:T(8,128)(2,1)}), bf16[4,32,384]{2,1,0:T(8,128)(2,1)S(1)}, u32[]{:S(2)}, u32[]{:S(2)}) async-start(bf16[4,32,384]{2,1,0:T(8,128)(2,1)} %broadcast_in_dim.17), calls=%async_computation.2 | async-start | bytes 196608 | tf_op jit(solution)/shard_map/all_to_all | solution.py:27
  54.5 24.6 %all-to-all-start = ((bf16[4,512,384]{1,2,0:T(8,128)(2,1)}), bf16[4,512,384]{1,2,0:T(8,128)(2,1)}, u32[]{:S(2)}, u32[]{:S(2)}) async-start(bf16[4,512,384]{1,2,0:T(8,128)(2,1)} %broadcast_in_dim.14), calls=%async_computation | async-start | bytes 3145728 | tf_op jit(solution)/shard_map/all_to_all | solution.py:27
  59.3 27.2 %copy-start.2 = (f32[512,96]{0,1:T(8,128)S(1)}, f32[512,96]{0,1:T(8,128)}, u32[]{:S(2)}) copy-start(f32[512,96]{0,1:T(8,128)} %param.13) | copy-start | bytes 589828
  80.0 54.1 %all-to-all-start.3 = ((bf16[32,32,384]{2,1,0:T(8,128)(2,1)}), bf16[32,32,384]{2,1,0:T(8,128)(2,1)}, u32[]{:S(2)}, u32[]{:S(2)}) async-start(bf16[32,32,384]{2,1,0:T(8,128)(2,1)} %broadcast_in_dim.18), calls=%async_computation.3 | async-start | bytes 1572864 | tf_op jit(solution)/shard_map/all_to_all | solution.py:27
  86.5 1.7 %copy-start.1 = (f32[4,512,384]{1,2,0:T(8,128)}, f32[4,512,384]{1,2,0:T(8,128)S(1)}, u32[]{:S(2)}) copy-start(f32[4,512,384]{1,2,0:T(8,128)S(1)} %convert_element_type.125) | copy-start | bytes 9437188
  86.5 3.4 %copy-start.4 = (f32[512]{0:T(512)S(1)}, f32[512]{0:T(512)}, u32[]{:S(2)}) copy-start(f32[512]{0:T(512)} %param.14) | copy-start | bytes 6148
  129.8 6.6 %copy-start.6 = (bf16[1024,96]{0,1:T(8,128)(2,1)S(1)}, bf16[1024,96]{0,1:T(8,128)(2,1)}, u32[]{:S(2)}) copy-start(bf16[1024,96]{0,1:T(8,128)(2,1)} %param.11) | copy-start | bytes 589828
where the time goes:
time: 147 us
  waiting for transfers between devices  39.6 us (27%)
  blocking collectives  35.2 us (24%)
  matrix products  23.3 us (16%)
  starting transfers between devices  21.8 us (15%)
  other arithmetic  17.3 us (12%)
  local copies, waits for them, and re-layouts  7.23 us (5%)
  between operations  2.19 us (1%)
    psum x4, blocking collectives, over_axes(): return functools.reduce(lax.psum, axes, shard)  35.2 us
    all_to_all x3, waiting for transfers between devices, from_everyone(): return lax.all_to_all(copies, axis, split_axis=0, concat_axis=0, tiled=True)  22.9 us
    all_to_all x1, waiting for transfers between devices, sent_and_summed(): lax.all_to_all(parts, axis, split_axis=0, concat_axis=0, tiled=True)  16.7 us
    all_to_all x3, starting transfers between devices, from_everyone(): return lax.all_to_all(copies, axis, split_axis=0, concat_axis=0, tiled=True)  14.3 us
    dot_general x1, matrix products, shards(): lax.dot_general(preact_grad, w_in, (((1,), (1,)), ((), ())), preferred_el...  10.3 us
    all_to_all x1, starting transfers between devices, sent_and_summed(): lax.all_to_all(parts, axis, split_axis=0, concat_axis=0, tiled=True)  7.44 us
    dot_general x1, matrix products, shards(): preact = jnp.dot(flat_rows, w_in, preferred_element_type=jnp.float32) + b_in  6.33 us
    reduce_sum x2, other arithmetic, energy(): jnp.sum(between * pair_weight[:, :, None], axis=1)  3.78 us
  transfers between devices with their start and end apart: 4, of which 3 were waited for; matrix products, arithmetic and copies ran while one was open for 10% of the time, Pallas kernels for 0%

commit v1 on v0

v1 whole, which is shorter than its diff:
```python
import functools

import jax
import jax.numpy as jnp
from jax import lax
from jax.experimental import pallas as pl
from jax.experimental.pallas import tpu as pltpu
from jax.sharding import Mesh
from jax.sharding import PartitionSpec as P

SPACE = ("x", "y", "c")
WIDE = ("x", "y", "m")

EPSILON = 1e-05
LOSS_SCALE = 4096.0
LANES = 128
VARS = 96
FOUR = 4
MEMBERS = 16
CELLS = 1024
HALF = CELLS // 2
NODE_TOTAL = 16384
PAIRS = float(MEMBERS * (MEMBERS - 1))
TRUTH_SCALE = 1.0 / (MEMBERS * VARS)
PAIR_SCALE = 1.0 / (PAIRS * VARS)

f32 = jnp.float32
bf16 = jnp.bfloat16


def vmem():
    return pl.BlockSpec(memory_space=pltpu.VMEM)


def forward_kernel(x_ref, w_ref, b_ref, wo_ref, extra_ref, preact_ref, pred_ref):
    total = extra_ref[...]
    units = w_ref.shape[1]
    step = 256
    for n in range(0, units, step):
        pre = jnp.dot(x_ref[...], w_ref[:, n : n + step], preferred_element_type=f32)
        pre = pre + b_ref[:, n : n + step]
        preact_ref[:, n : n + step] = pre
        half = 0.5 * pre
        act = (half + half * jnp.tanh(half)).astype(bf16)
        total = total + jnp.dot(act, wo_ref[n : n + step, :], preferred_element_type=f32)
    pred_ref[...] = total.astype(bf16)


def forward(flat, w_in, b_in, w_pad, extra, nodes):
    rows = 256
    tiles = nodes // rows
    width, units = w_in.shape
    return pl.pallas_call(
        forward_kernel,
        grid=(FOUR, tiles),
        in_specs=[
            pl.BlockSpec((rows, width), lambda j, t: (j * tiles + t, 0)),
            pl.BlockSpec((width, units), lambda j, t: (0, 0)),
            pl.BlockSpec((1, units), lambda j, t: (0, 0)),
            pl.BlockSpec((units, LANES), lambda j, t: (0, 0)),
            pl.BlockSpec((rows, LANES), lambda j, t: (t, j)),
        ],
        out_specs=[
            pl.BlockSpec((rows, units), lambda j, t: (j * tiles + t, 0)),
            pl.BlockSpec((rows, LANES), lambda j, t: (t, j)),
        ],
        out_shape=[
            jax.ShapeDtypeStruct((FOUR * nodes, units), f32),
            jax.ShapeDtypeStruct((nodes, FOUR * LANES), bf16),
        ],
        cost_estimate=pl.CostEstimate(
            flops=2 * FOUR * nodes * width * units, bytes_accessed=16 << 20, transcendentals=0
        ),
        name="forward",
    )(flat, w_in, b_in, w_pad, extra)


def cells_kernel(base, row_ref, pred_ref, out_ref):
    nodes = pred_ref.shape[0]
    ids = lax.broadcasted_iota(jnp.int32, (HALF, nodes), 0) + base
    picker = jnp.where(ids == row_ref[...], 1.0, 0.0).astype(bf16)
    out_ref[...] = jnp.dot(picker, pred_ref[...], preferred_element_type=f32).astype(out_ref.dtype)


def cell_sums(row, pred, base, dtype):
    return pl.pallas_call(
        functools.partial(cells_kernel, base),
        in_specs=[vmem(), vmem()],
        out_specs=vmem(),
        out_shape=jax.ShapeDtypeStruct((HALF, pred.shape[1]), dtype),
        cost_estimate=pl.CostEstimate(
            flops=2 * HALF * pred.size, bytes_accessed=2 << 20, transcendentals=0
        ),
        name="cells",
    )(row, pred)


def fine_kernel(place_ref, got_ref, truth_ref, area_ref, grad_ref, loss_ref, part, slope):
    for k in range(MEMBERS):
        block = got_ref[k // FOUR, :, (k % FOUR) * LANES : (k % FOUR + 1) * LANES]
        part[k] = block.astype(f32).T[:VARS, :]
    start = pl.multiple_of(place_ref[0] * LANES, LANES)
    truth = truth_ref[:, pl.ds(start, LANES)]
    area = area_ref[:, pl.ds(start, LANES)]
    slope[:, VARS:, :] = jnp.zeros((MEMBERS, LANES - VARS, LANES), f32)

    def member(m, carry):
        truths, pairs = carry
        own = part[m]
        off = own - truth
        mean = jnp.sum(off * off, axis=0, keepdims=True) * (1.0 / VARS) + EPSILON
        inverse = lax.rsqrt(mean)
        truths = truths + mean * inverse
        total = jnp.zeros_like(own)
        for k in range(MEMBERS):
            between = own - part[k]
            mean = jnp.sum(between * between, axis=0, keepdims=True) * (1.0 / VARS) + EPSILON
            weight = lax.rsqrt(mean)
            distinct = jnp.where(m == k, 0.0, 1.0)
            pairs = pairs + (mean * weight) * distinct
            total = total + between * weight
        slope[m, :VARS, :] = off * (inverse * area * TRUTH_SCALE) - total * (area * PAIR_SCALE)
        return truths, pairs

    zero = jnp.zeros((1, LANES), f32)
    truths, pairs = lax.fori_loop(0, MEMBERS, member, (zero, zero))
    loss_ref[...] = area * (truths * (1.0 / MEMBERS) - pairs * (0.5 / PAIRS))
    for k in range(MEMBERS):
        grad_ref[k // FOUR, :, (k % FOUR) * LANES : (k % FOUR + 1) * LANES] = slope[k].T.astype(bf16)


def fine(place, got, truth, area):
    return pl.pallas_call(
        fine_kernel,
        in_specs=[pl.BlockSpec(memory_space=pltpu.SMEM), vmem(), vmem(), vmem()],
        out_specs=[vmem(), vmem()],
        out_shape=[
            jax.ShapeDtypeStruct(got.shape, bf16),
            jax.ShapeDtypeStruct((1, LANES), f32),
        ],
        scratch_shapes=[
            pltpu.VMEM((MEMBERS, VARS, LANES), f32),
            pltpu.VMEM((MEMBERS, LANES, LANES), f32),
        ],
        cost_estimate=pl.CostEstimate(
            flops=MEMBERS * MEMBERS * VARS * LANES * 16, bytes_accessed=2 << 20, transcendentals=0
        ),
        name="fine",
    )(place, got, truth, area)


def three(value):
    high = value.astype(bf16).astype(f32)
    rest = value - high
    middle = rest.astype(bf16).astype(f32)
    return high, middle, rest - middle


def coarse_kernel(got_ref, loss_ref, area_ref, out_ref):
    places = got_ref.shape[0] // FOUR
    lane = lax.broadcasted_iota(jnp.int32, (8, LANES), 1)
    rank = lax.broadcasted_iota(jnp.int32, (8, LANES), 0)
    real = lane < VARS
    spare = lane >= VARS + 24
    sums = []
    for m in range(FOUR):
        total = got_ref[m].astype(f32)
        for s in range(1, places):
            total = total + got_ref[s * FOUR + m].astype(f32)
        sums += [total[:, j * LANES : (j + 1) * LANES] for j in range(FOUR)]

    def across(value):
        return jnp.sum(value, axis=1, keepdims=True)

    counts = across(jnp.where(spare, sums[0] + sums[1], 0.0))
    weight = across(jnp.where(spare, sums[2], 0.0))
    inverse = 1.0 / jnp.maximum(counts, 1.0)
    truth = jnp.zeros((8, LANES), f32)
    for j in range(FOUR):
        turned = pltpu.roll(sums[j], (24 * j - VARS) % LANES, 1)
        truth = jnp.where((lane >= 24 * j) & (lane < 24 * (j + 1)), turned, truth)
    truth = truth * inverse
    means = [jnp.where(real, (v * inverse).astype(bf16).astype(f32), 0.0) for v in sums]
    truths = jnp.zeros((8, 1), f32)
    pairs = jnp.zeros((8, 1), f32)
    grads = []
    for m in range(MEMBERS):
        off = means[m] - truth
        mean = across(off * off) * (1.0 / VARS) + EPSILON
        turn = lax.rsqrt(mean)
        truths = truths + mean * turn
        grads.append(off * (turn * TRUTH_SCALE))
    for m in range(MEMBERS):
        for k in range(m):
            between = means[m] - means[k]
            mean = across(between * between) * (1.0 / VARS) + EPSILON
            turn = lax.rsqrt(mean)
            pairs = pairs + mean * turn
            pull = between * (turn * PAIR_SCALE)
            grads[m] = grads[m] - pull
            grads[k] = grads[k] + pull
    loss = jnp.sum(weight * (truths * (1.0 / MEMBERS) - pairs * (1.0 / PAIRS)), axis=0, keepdims=True)
    fine_loss = across(loss_ref[...])
    area = across(area_ref[...])
    pieces = jnp.zeros((8, LANES), f32)
    for index, value in enumerate((*three(fine_loss), *three(loss), *three(area))):
        pieces = jnp.where(lane == VARS + index, value, pieces)
    pieces = jnp.where(rank == 0, pieces, 0.0)
    scale = weight * inverse
    for m in range(FOUR):
        rows = [grads[m * FOUR + j] * scale for j in range(FOUR)]
        rows[0] = rows[0] + pieces
        block = jnp.concatenate(rows, axis=1).astype(bf16)
        for s in range(places):
            out_ref[s * FOUR + m] = block


def coarse(got, loss, area):
    return pl.pallas_call(
        coarse_kernel,
        in_specs=[vmem(), vmem(), vmem()],
        out_specs=vmem(),
        out_shape=jax.ShapeDtypeStruct(got.shape, bf16),
        cost_estimate=pl.CostEstimate(flops=1 << 21, bytes_accessed=1 << 20, transcendentals=0),
        name="coarse",
    )(got, loss, area)


def picked(base, column, table):
    ids = lax.broadcasted_iota(jnp.int32, (column.shape[0], HALF), 1) + base
    wide = jnp.concatenate([column] * (HALF // LANES), axis=1)
    picker = jnp.where(ids == wide, 1.0, 0.0).astype(bf16)
    return jnp.dot(picker, table, preferred_element_type=f32)


def near_kernel(column_ref, table_ref, out_ref):
    out_ref[...] = picked(0, column_ref[...], table_ref[...])


def near(column, table):
    return pl.pallas_call(
        near_kernel,
        in_specs=[vmem(), vmem()],
        out_specs=vmem(),
        out_shape=jax.ShapeDtypeStruct((column.shape[0], table.shape[1]), f32),
        cost_estimate=pl.CostEstimate(
            flops=2 * HALF * column.shape[0] * table.shape[1], bytes_accessed=2 << 20, transcendentals=0
        ),
        name="near",
    )(column, table)


def far_kernel(column_ref, near_ref, fine_ref, own_ref, other_ref, up_ref, factor_ref, score_ref):
    total = near_ref[...] + picked(HALF, column_ref[...], other_ref[...])
    up_ref[...] = (total + fine_ref[...].astype(f32)).astype(bf16)
    sums = own_ref[:, :LANES].astype(f32) + other_ref[:, :LANES].astype(f32)
    sums = jnp.sum(sums, axis=0, keepdims=True)
    lane = lax.broadcasted_iota(jnp.int32, (1, LANES), 1)

    def of(index):
        here = (lane >= VARS + 3 * index) & (lane < VARS + 3 * index + 3)
        return jnp.sum(jnp.where(here, sums, 0.0), axis=1, keepdims=True)

    area = of(2) * (1.0 / FOUR)
    factor_ref[...] = jnp.broadcast_to(LOSS_SCALE * NODE_TOTAL / area, (1, LANES))
    score_ref[0] = (of(0) / area)[0, 0]
    score_ref[1] = (of(1) / area)[0, 0]


def far(column, near_part, fine_part, own, other):
    return pl.pallas_call(
        far_kernel,
        in_specs=[vmem()] * 5,
        out_specs=[vmem(), vmem(), pl.BlockSpec(memory_space=pltpu.SMEM)],
        out_shape=[
            jax.ShapeDtypeStruct(fine_part.shape, bf16),
            jax.ShapeDtypeStruct((1, LANES), f32),
            jax.ShapeDtypeStruct((2,), f32),
        ],
        name="far",
    )(column, near_part, fine_part, own, other)


def backward_kernel(up_ref, preact_ref, wo_ref, w_ref, factor_ref, out_ref):
    units = w_ref.shape[1]
    step = 256
    total = None
    for n in range(0, units, step):
        hidden = jnp.dot(up_ref[...], wo_ref[:, n : n + step], preferred_element_type=f32)
        pre = preact_ref[:, n : n + step]
        half = 0.5 * pre
        sigma = 0.5 * jnp.tanh(half) + 0.5
        slope = sigma * (1.0 + pre * (1.0 - sigma))
        grad = (hidden * slope).astype(bf16)
        more = lax.dot_general(
            grad, w_ref[:, n : n + step], (((1,), (1,)), ((), ())), preferred_element_type=f32
        )
        total = more if total is None else total + more
    out_ref[...] = (total * factor_ref[0:1, 0:1]).astype(bf16)


def backward(up, preact, wo_t, w_in, factor, nodes):
    rows = 256
    tiles = nodes // rows
    width, units = w_in.shape
    return pl.pallas_call(
        backward_kernel,
        grid=(FOUR, tiles),
        in_specs=[
            pl.BlockSpec((rows, LANES), lambda j, t: (t, j)),
            pl.BlockSpec((rows, units), lambda j, t: (j * tiles + t, 0)),
            pl.BlockSpec((LANES, units), lambda j, t: (0, 0)),
            pl.BlockSpec((width, units), lambda j, t: (0, 0)),
            pl.BlockSpec((1, LANES), lambda j, t: (0, 0)),
        ],
        out_specs=pl.BlockSpec((rows, width), lambda j, t: (j * tiles + t, 0)),
        out_shape=jax.ShapeDtypeStruct((FOUR * nodes, width), bf16),
        cost_estimate=pl.CostEstimate(
            flops=2 * FOUR * nodes * width * units, bytes_accessed=16 << 20, transcendentals=0
        ),
        name="backward",
    )(up, preact, wo_t, w_in, factor)


def features(target, area, nodes):
    turn = jnp.arange(nodes, dtype=jnp.int32)[:, None]
    eight = jnp.arange(8, dtype=jnp.int32)[None, :]
    low = (turn % 16 == eight).astype(f32)
    high = (turn % 16 == eight + 8).astype(f32)
    spread = jnp.where(turn % 8 == eight, area[:, None], 0.0)
    return (low, high, spread, jnp.zeros_like(spread))


def shards(latent, w_in, b_in, w_out, b_out, target, area, cell_of):
    members, nodes, width = latent.shape
    flat = latent.reshape(members * nodes, width)
    spare = LANES - VARS
    w_pad = jnp.pad(w_out, ((0, 0), (0, spare)))
    wo_t = jnp.pad(w_out.T, ((0, spare), (0, 0)))
    bias = jnp.broadcast_to(b_out[None, :], (nodes, VARS))
    last = features(target, area, nodes)
    pieces = []
    for j in range(FOUR):
        pieces += [bias, target[:, 24 * j : 24 * (j + 1)], last[j]]
    extra = jnp.concatenate(pieces, axis=1)
    cell = jnp.bitwise_xor(cell_of, lax.axis_index("c") * HALF)
    row = cell[None, :]
    column = jnp.broadcast_to(cell[:, None], (nodes, LANES))
    area_row = area[None, :]
    place = lax.axis_index("m").astype(jnp.int32)[None]

    preact, pred = forward(flat, w_in, b_in[None, :], w_pad, extra, nodes)
    swap = [(0, 1), (1, 0)]
    sent = cell_sums(row, pred, HALF, bf16)
    arrived = lax.ppermute(sent, "c", swap)
    kept = cell_sums(row, pred, 0, f32)
    both = (kept + arrived.astype(f32)).astype(bf16).reshape(64, 8, FOUR * LANES)
    gathered = lax.all_to_all(both, WIDE, 0, 0, tiled=True)
    everyone = lax.all_to_all(pred.reshape(FOUR, LANES, FOUR * LANES), "m", 0, 0, tiled=True)
    fine_grad, fine_loss = fine(place, everyone, target.T, area_row)
    table = coarse(gathered, fine_loss, area_row)
    own = lax.all_to_all(table, WIDE, 0, 0, tiled=True).reshape(HALF, FOUR * LANES)
    fine_part = lax.all_to_all(fine_grad, "m", 0, 0, tiled=True).reshape(nodes, FOUR * LANES)
    other = lax.ppermute(own, "c", swap)
    near_part = near(column, own)
    up, factor, scores = far(column, near_part, fine_part, own, other)
    latent_grad = backward(up, preact, wo_t, w_in, factor, nodes)
    return (latent_grad.reshape(members, nodes, width), scores)


def solution(mesh):
    split = Mesh(mesh.devices.reshape(4, 4, 2, mesh.shape["member"]), ("x", "y", "c", "m"))
    return jax.shard_map(
        shards,
        mesh=split,
        in_specs=(P("m", SPACE, None), P(), P(), P(), P(), P(SPACE, None), P(SPACE), P(SPACE)),
        out_specs=(P("m", SPACE, None), P()),
        check_vma=False,
    )
```

time: 147 us -> 116 us (0.79)
  Pallas kernels: 0 us -> 47.3 us
  matrix products: 23.3 us -> 0 us
  waiting for transfers between devices: 39.6 us -> 19.1 us
  blocking collectives: 35.2 us -> 16.8 us
  other arithmetic: 17.3 us -> 4.5 us
  starting transfers between devices: 21.8 us -> 17.4 us
  local copies, waits for them, and re-layouts: 7.23 us -> 9.02 us
    pallas_call x0 -> x8, Pallas kernels: none -> 47.3 us  [the longest x1 16.3 us: forward(): pl.pallas_call(forward_kernel, grid=(FOUR, tiles), in_specs=[pl.BlockSpec...]
    psum x4 -> x0, blocking collectives: 35.2 us -> none  [over_axes(): return functools.reduce(lax.psum, axes, shard)]
    dot_general x6 -> x0, matrix products: 23.3 us -> none  [the longest x1 10.3 us: shards(): lax.dot_general(preact_grad, w_in, (((1,), (1,)), ((), ())), preferred_el...]
    all_to_all x4 -> x3, waiting for transfers between devices: 39.6 us -> 19.1 us  [the longest x1 7.38 us: shards(): gathered = lax.all_to_all(both, WIDE, 0, 0, tiled=True)]
    all_to_all x0 -> x1, blocking collectives: none -> 16.8 us  [shards(): lax.all_to_all(table, WIDE, 0, 0, tiled=True).reshape(HALF, FOUR * LANES)]
    reduce_sum x10 -> x0, other arithmetic: 8.92 us -> none  [the longest x2 3.78 us: energy(): jnp.sum(between * pair_weight[:, :, None], axis=1)]
    all_to_all x4 -> x3, starting transfers between devices: 21.8 us -> 17.4 us  [the longest x1 8.54 us: shards(): gathered = lax.all_to_all(both, WIDE, 0, 0, tiled=True)]
    convert_element_type x6 -> x1, other arithmetic: 3.5 us -> 0.13 us  [features(): high = (turn % 16 == eight + 8).astype(f32)]
  transfers between devices with their start and end apart: 4 -> 5, of which waited for: 3 -> 3; matrix products, arithmetic and copies ran while one was open for 10% -> 3% of each run, Pallas kernels for 0% -> 9%
where the time goes in v1:
time: 116 us; the launch traced here: 115 us
  Pallas kernels  47.3 us (41%)
  waiting for transfers between devices  19.1 us (16%)
  starting transfers between devices  17.4 us (15%)
  blocking collectives  16.8 us (14%)
  local copies, waits for them, and re-layouts  9.02 us (8%)
  other arithmetic  4.5 us (4%)
    all_to_all x1, blocking collectives, shards(): lax.all_to_all(table, WIDE, 0, 0, tiled=True).reshape(HALF, FOUR * LANES)  16.8 us
    pallas_call x1, Pallas kernels, forward(): pl.pallas_call(forward_kernel, grid=(FOUR, tiles), in_specs=[pl.BlockSpec...  16.3 us
    pallas_call x1, Pallas kernels, backward(): pl.pallas_call(backward_kernel, grid=(FOUR, tiles), in_specs=[pl.BlockSpe...  13.1 us
    all_to_all x1, starting transfers between devices, shards(): gathered = lax.all_to_all(both, WIDE, 0, 0, tiled=True)  8.54 us
    all_to_all x1, waiting for transfers between devices, shards(): gathered = lax.all_to_all(both, WIDE, 0, 0, tiled=True)  7.38 us
    all_to_all x1, waiting for transfers between devices, shards(): lax.all_to_all(fine_grad, 'm', 0, 0, tiled=True)  6.29 us
    all_to_all x1, starting transfers between devices, shards(): lax.all_to_all(pred.reshape(FOUR, LANES, FOUR * LANES), 'm', 0, 0, tiled=...  5.43 us
    all_to_all x1, waiting for transfers between devices, shards(): lax.all_to_all(pred.reshape(FOUR, LANES, FOUR * LANES), 'm', 0, 0, tiled=...  5.42 us
  transfers between devices with their start and end apart: 5, of which 3 were waited for; matrix products, arithmetic and copies ran while one was open for 3% of the time, Pallas kernels for 9%

profile of v1, /device:TPU:0, one launch (start us, length us, event | category | flops | bytes accessed | tf_op | source)
XLA Modules:
  0.0 115.0 jit_solution(5963360699021140981)
XLA Ops:
  0.7 0.9 fusion.9
  1.7 0.1 copy.24
  1.8 0.1 copy.23
  2.0 0.1 copy.22
  2.1 1.1 copy.15
  3.2 1.3 %broadcast_xor_fusion = s32[512]{0:T(512)} fusion(s32[512]{0:T(512)} %param.15, s32[]{:T(128)S(6)} %mul.3), kind=kLoop, calls=%fused_computation.17 | loop fusion | flops 512 | bytes 4100 | tf_op jit(solution)/shard_map/xor | solution.py:346
  4.5 0.9 fusion.2
  5.4 0.8 pad.8.wo_ref
  6.1 0.1 compare_convert_fusion
  6.3 0.7 broadcast_in_dim.43
  7.0 1.7 %concatenate.3.extra_ref = f32[512,512]{1,0:T(8,128)} concatenate(f32[512,96]{1,0:T(8,128)S(1)} %broadcast_in_dim.43, f32[512,24]{1,0:T(8,128)S(1)} %copy.22, f32[512,8]{1,0:T(8,128)S(1)} %get-tuple-element.21, f32[512,96]{1,0:T(8,128)S(1)} %broadcast_in_dim.43, f32[512,24]{1,0:T(8,128)S(1)} %copy.23, f32[512,8]{1,0:T(8,128)S(1)} %get-tuple-element.20, ...), dimensions={1} | concatenate | bytes 2097152 | tf_op jit(solution)/shard_map/concatenate | solution.py:345
  8.7 16.3 %forward.1 = (f32[2048,1024]{1,0:T(8,128)}, bf16[512,512]{1,0:T(8,128)(2,1)}) custom-call(bf16[2048,1024]{1,0:T(8,128)(2,1)} %bitcast.24, bf16[1024,1024]{1,0:T(8,128)(2,1)} %w_ref.3, f32[1,1024]{1,0:T(1,128)} %bitcast.25, bf16[1024,128]{1,0:T(8,128)(2,1)} %pad.8.wo_ref, f32[512,512]{1,0:T(8,128)} %concatenate.3.extra_ref), custom_call_target="tpu_custom_call" | custom-call | flops 4294967296 | bytes 16777216 | tf_op jit(solution)/shard_map/forward/pallas_call | solution.py:53
  25.0 2.3 %cells.3 = bf16[512,512]{1,0:T(8,128)(2,1)} custom-call(s32[1,512]{1,0:T(1,128)} %bitcast.20, bf16[512,512]{1,0:T(8,128)(2,1)} %get-tuple-element.9.pred_ref), custom_call_target="tpu_custom_call" | custom-call | flops 268435456 | bytes 2097152 | tf_op jit(solution)/shard_map/cells/pallas_call | solution.py:86
  27.3 5.4 %all-to-all-start.1 = ((bf16[4,128,512]{2,1,0:T(8,128)(2,1)}), bf16[4,128,512]{2,1,0:T(8,128)(2,1)S(1)}, u32[]{:S(2)}, u32[]{:S(2)}) async-start(bf16[4,128,512]{2,1,0:T(8,128)(2,1)} %bitcast.16), calls=%async_computation.1 | async-start | bytes 1048576 | tf_op jit(solution)/shard_map/all_to_all | solution.py:359
  32.7 2.5 %cells.2 = f32[512,512]{1,0:T(8,128)} custom-call(s32[1,512]{1,0:T(1,128)} %bitcast.21, bf16[512,512]{1,0:T(8,128)(2,1)} %get-tuple-element.9.pred_ref), custom_call_target="tpu_custom_call" | custom-call | flops 268435456 | bytes 2097152 | tf_op jit(solution)/shard_map/cells/pallas_call | solution.py:86
  35.3 2.2 %fusion = bf16[64,8,512]{2,1,0:T(8,128)(2,1)} fusion(f32[512,512]{1,0:T(8,128)} %cells.2, bf16[512,512]{1,0:T(8,128)(2,1)S(1)} %collective-permute-done), kind=kLoop, calls=%fused_computation.1 | loop fusion | flops 786432 | bytes 2097152 | tf_op jit(solution)/shard_map/reshape | solution.py:357
  37.5 5.4 %all-to-all-done.1.got_ref = bf16[4,128,512]{2,1,0:T(8,128)(2,1)S(1)} async-done(((bf16[4,128,512]{2,1,0:T(8,128)(2,1)}), bf16[4,128,512]{2,1,0:T(8,128)(2,1)S(1)}, u32[]{:S(2)}, u32[]{:S(2)}) %all-to-all-start.1) | async-done | bytes 524320 | tf_op jit(solution)/shard_map/all_to_all | solution.py:359
  42.9 8.5 %all-to-all-start = ((bf16[64,8,512]{2,1,0:T(8,128)(2,1)}), bf16[64,8,512]{2,1,0:T(8,128)(2,1)S(1)}, u32[]{:S(2)}, u32[]{:S(2)}) async-start(bf16[64,8,512]{2,1,0:T(8,128)(2,1)} %fusion), calls=%async_computation | async-start | bytes 1048576 | tf_op jit(solution)/shard_map/all_to_all | solution.py:358
  51.5 5.2 %fine.1 = (bf16[4,128,512]{2,1,0:T(8,128)(2,1)}, f32[1,128]{1,0:T(1,128)}) custom-call(s32[1]{0:T(128)} %bitcast.4.place_ref, bf16[4,128,512]{2,1,0:T(8,128)(2,1)} %copy-done.1, f32[96,512]{1,0:T(8,128)} %bitcast.19, f32[1,512]{1,0:T(1,128)} %bitcast.22), custom_call_target="tpu_custom_call" | custom-call | flops 50331648 | bytes 2097152 | tf_op jit(solution)/shard_map/fine/pallas_call | solution.py:133
  56.7 7.4 %all-to-all-done.got_ref = bf16[64,8,512]{2,1,0:T(8,128)(2,1)S(1)} async-done(((bf16[64,8,512]{2,1,0:T(8,128)(2,1)}), bf16[64,8,512]{2,1,0:T(8,128)(2,1)S(1)}, u32[]{:S(2)}, u32[]{:S(2)}) %all-to-all-start) | async-done | bytes 524320 | tf_op jit(solution)/shard_map/all_to_all | solution.py:358
  64.1 0.8 copy-done.2
  64.9 2.3 %coarse.1 = bf16[64,8,512]{2,1,0:T(8,128)(2,1)} custom-call(bf16[64,8,512]{2,1,0:T(8,128)(2,1)} %copy-done.2, f32[1,128]{1,0:T(1,128)} %get-tuple-element.10.loss_ref, f32[1,512]{1,0:T(1,128)} %bitcast.23), custom_call_target="tpu_custom_call" | custom-call | flops 2097152 | bytes 1048576 | tf_op jit(solution)/shard_map/coarse/pallas_call | solution.py:219
  67.2 16.8 %all_to_all.20 = bf16[64,8,512]{2,1,0:T(8,128)(2,1)S(1)} all-to-all(bf16[64,8,512]{2,1,0:T(8,128)(2,1)} %coarse.1), channel_id=1, replica_groups=mesh['x'=4,'y'=4,'c'=2,'m'=4] {'x','y','m'}, dimensions={0} | all-to-all | bytes 1048576 | tf_op jit(solution)/shard_map/all_to_all | solution.py:362
  84.0 3.5 %all-to-all-start.3 = ((bf16[4,128,512]{2,1,0:T(8,128)(2,1)}), bf16[4,128,512]{2,1,0:T(8,128)(2,1)S(1)}, u32[]{:S(2)}, u32[]{:S(2)}) async-start(bf16[4,128,512]{2,1,0:T(8,128)(2,1)} %get-tuple-element.11), calls=%async_computation.3 | async-start | bytes 1048576 | tf_op jit(solution)/shard_map/all_to_all | solution.py:363
  87.5 0.7 pad.9.wo_ref
  88.2 0.8 broadcast_in_dim.40.column_ref
  89.0 2.5 %near.1.near_ref = f32[512,512]{1,0:T(8,128)} custom-call(s32[512,128]{1,0:T(8,128)} %broadcast_in_dim.40.column_ref, bf16[512,512]{1,0:T(8,128)(2,1)} %bitcast.14), custom_call_target="tpu_custom_call" | custom-call | flops 268435456 | bytes 2097152 | tf_op jit(solution)/shard_map/near/pallas_call | solution.py:241
  91.6 6.3 %all-to-all-done.3 = bf16[4,128,512]{2,1,0:T(8,128)(2,1)S(1)} async-done(((bf16[4,128,512]{2,1,0:T(8,128)(2,1)}), bf16[4,128,512]{2,1,0:T(8,128)(2,1)S(1)}, u32[]{:S(2)}, u32[]{:S(2)}) %all-to-all-start.3) | async-done | bytes 524320 | tf_op jit(solution)/shard_map/all_to_all | solution.py:363
  97.9 0.8 copy-done.3
  98.7 0.2 copy-done.5
  98.8 3.0 %far.1 = (bf16[512,512]{1,0:T(8,128)(2,1)}, f32[1,128]{1,0:T(1,128)}, f32[2]{0:T(128)}) custom-call(s32[512,128]{1,0:T(8,128)} %broadcast_in_dim.40.column_ref, f32[512,512]{1,0:T(8,128)} %near.1.near_ref, bf16[512,512]{1,0:T(8,128)(2,1)} %bitcast.17, bf16[512,512]{1,0:T(8,128)(2,1)} %bitcast.15, bf16[512,512]{1,0:T(8,128)(2,1)} %copy-done.5), custom_call_target="tpu_custom_call" | custom-call | tf_op jit(solution)/shard_map/far/pallas_call | solution.py:271
  101.9 13.1 %backward.1 = bf16[2048,1024]{1,0:T(8,128)(2,1)} custom-call(bf16[512,512]{1,0:T(8,128)(2,1)} %get-tuple-element.12.up_ref, f32[2048,1024]{1,0:T(8,128)} %get-tuple-element.13.preact_ref, bf16[128,1024]{1,0:T(8,128)(2,1)} %pad.9.wo_ref, bf16[1024,1024]{1,0:T(8,128)(2,1)} %w_ref.3, f32[1,128]{1,0:T(1,128)} %get-tuple-element.14.factor_ref), custom_call_target="tpu_custom_call" | custom-call | flops 4294967296 | bytes 16777216 | tf_op jit(solution)/shard_map/backward/pallas_call | solution.py:306
  (20 shorter events, 0.2 us)
Async XLA Ops:
  27.3 8.0 %collective-permute-start = (bf16[512,512]{1,0:T(8,128)(2,1)}, bf16[512,512]{1,0:T(8,128)(2,1)S(1)}, u32[]{:S(2)}, u32[]{:S(2)}) collective-permute-start(bf16[512,512]{1,0:T(8,128)(2,1)} %cells.3), channel_id=1, source_target_pairs={{0,4},{4,0},{1,5},{5,1},{2,6},{6,2},{3,7},{7,3},{8,12},{12,8},{9,1... | collective-permute-start | bytes 1572872 | tf_op jit(solution)/shard_map/ppermute | solution.py:355
  27.3 15.6 %all-to-all-start.1 = ((bf16[4,128,512]{2,1,0:T(8,128)(2,1)}), bf16[4,128,512]{2,1,0:T(8,128)(2,1)S(1)}, u32[]{:S(2)}, u32[]{:S(2)}) async-start(bf16[4,128,512]{2,1,0:T(8,128)(2,1)} %bitcast.16), calls=%async_computation.1 | async-start | bytes 1048576 | tf_op jit(solution)/shard_map/all_to_all | solution.py:359
  32.7 54.7 %copy-start.4 = (bf16[1024,96]{0,1:T(8,128)(2,1)S(1)}, bf16[1024,96]{0,1:T(8,128)(2,1)}, u32[]{:S(2)}) copy-start(bf16[1024,96]{0,1:T(8,128)(2,1)} %param.11) | copy-start | bytes 589828
  32.7 55.5 %copy-start.6 = (s32[512]{0:T(512)S(1)}, s32[512]{0:T(512)}, u32[]{:S(2)}) copy-start(s32[512]{0:T(512)} %broadcast_xor_fusion) | copy-start | bytes 6148
  42.9 8.6 %copy-start.1 = (bf16[4,128,512]{2,1,0:T(8,128)(2,1)}, bf16[4,128,512]{2,1,0:T(8,128)(2,1)S(1)}, u32[]{:S(2)}) copy-start(bf16[4,128,512]{2,1,0:T(8,128)(2,1)S(1)} %all-to-all-done.1.got_ref) | copy-start | bytes 1572868
  42.9 21.2 %all-to-all-start = ((bf16[64,8,512]{2,1,0:T(8,128)(2,1)}), bf16[64,8,512]{2,1,0:T(8,128)(2,1)S(1)}, u32[]{:S(2)}, u32[]{:S(2)}) async-start(bf16[64,8,512]{2,1,0:T(8,128)(2,1)} %fusion), calls=%async_computation | async-start | bytes 1048576 | tf_op jit(solution)/shard_map/all_to_all | solution.py:358
  64.1 0.8 copy-start.2
  84.0 5.1 %copy-start = (bf16[64,8,512]{2,1,0:T(8,128)(2,1)}, bf16[64,8,512]{2,1,0:T(8,128)(2,1)S(1)}, u32[]{:S(2)}) copy-start(bf16[64,8,512]{2,1,0:T(8,128)(2,1)S(1)} %all_to_all.20) | copy-start | bytes 1572868
  84.0 13.9 %collective-permute-start.1 = (bf16[512,512]{1,0:T(8,128)(2,1)S(1)}, bf16[512,512]{1,0:T(8,128)(2,1)S(1)}, u32[]{:S(2)}, u32[]{:S(2)}) collective-permute-start(bf16[512,512]{1,0:T(8,128)(2,1)S(1)} %bitcast.13), channel_id=1, source_target_pairs={{0,4},{4,0},{1,5},{5,1},{2,6},{6,2},{3,7},{7,3},{8,12},{12,8},{9,1... | collective-permute-start | bytes 1572872 | tf_op jit(solution)/shard_map/ppermute | solution.py:364
  84.0 13.9 %all-to-all-start.3 = ((bf16[4,128,512]{2,1,0:T(8,128)(2,1)}), bf16[4,128,512]{2,1,0:T(8,128)(2,1)S(1)}, u32[]{:S(2)}, u32[]{:S(2)}) async-start(bf16[4,128,512]{2,1,0:T(8,128)(2,1)} %get-tuple-element.11), calls=%async_computation.3 | async-start | bytes 1048576 | tf_op jit(solution)/shard_map/all_to_all | solution.py:363
  97.9 0.8 copy-start.3
  97.9 1.0 copy-start.5

commit v2 on v1

v2 whole, which is shorter than its diff:
```python
import functools

import jax
import jax.numpy as jnp
from jax import lax
from jax.experimental import pallas as pl
from jax.experimental.pallas import tpu as pltpu
from jax.sharding import Mesh
from jax.sharding import PartitionSpec as P

SPACE = ("x", "y", "c")
WIDE = ("x", "y", "m")

EPSILON = 1e-05
LOSS_SCALE = 4096.0
LANES = 128
VARS = 96
FOUR = 4
MEMBERS = 16
CELLS = 1024
HALF = CELLS // 2
NODE_TOTAL = 16384
PAIRS = float(MEMBERS * (MEMBERS - 1))
TRUTH_SCALE = 1.0 / (MEMBERS * VARS)
PAIR_SCALE = 1.0 / (PAIRS * VARS)

f32 = jnp.float32
bf16 = jnp.bfloat16


def vmem():
    return pl.BlockSpec(memory_space=pltpu.VMEM)


def fits(mib):
    return pltpu.CompilerParams(vmem_limit_bytes=mib << 20)


def smem():
    return pl.BlockSpec(memory_space=pltpu.SMEM)


def forward_kernel(
    x_ref, w_ref, b_ref, wo_ref, bo_ref, truth_ref, area_ref, preact_ref, pred_ref, wide, bias, extra
):
    j = pl.program_id(0)
    nodes = x_ref.shape[0]
    spare = LANES - VARS

    @pl.when(j == 0)
    def _():
        wide[:VARS, :] = wo_ref[...]
        wide[VARS:, :] = jnp.zeros((spare, wide.shape[1]), bf16)
        bias[...] = jnp.zeros_like(bias)
        bias[:, :VARS] = bo_ref[...]
        extra[:VARS, :] = jnp.zeros((VARS, nodes), f32)

    lane = lax.broadcasted_iota(jnp.int32, (8, nodes), 1)
    rank = lax.broadcasted_iota(jnp.int32, (8, nodes), 0)
    ones = jnp.where((lane & 15) == rank + 8 * j, 1.0, 0.0)
    spread = jnp.where((lane & 7) == rank, area_ref[...], 0.0)
    extra[VARS : VARS + 24, :] = truth_ref[pl.ds(pl.multiple_of(24 * j, 8), 24), :]
    extra[VARS + 24 :, :] = jnp.where(j < 2, ones, jnp.where(j == 2, spread, 0.0))
    pre = jnp.dot(x_ref[...], w_ref[...], preferred_element_type=f32) + b_ref[...]
    preact_ref[...] = pre
    half = 0.5 * pre
    act = (half + half * jnp.tanh(half)).astype(bf16)
    total = lax.dot_general(act, wide[...], (((1,), (1,)), ((), ())), preferred_element_type=f32)
    pred_ref[...] = (total + bias[...] + extra[...].T).astype(bf16)


def forward(flat, w_in, b_in, wo_t, b_out, truth, area, nodes):
    width, units = w_in.shape
    return pl.pallas_call(
        forward_kernel,
        grid=(FOUR,),
        in_specs=[
            pl.BlockSpec((nodes, width), lambda j: (j, 0)),
            pl.BlockSpec((width, units), lambda j: (0, 0)),
            pl.BlockSpec((1, units), lambda j: (0, 0)),
            pl.BlockSpec((VARS, units), lambda j: (0, 0)),
            pl.BlockSpec((1, VARS), lambda j: (0, 0)),
            pl.BlockSpec((VARS, nodes), lambda j: (0, 0)),
            pl.BlockSpec((1, nodes), lambda j: (0, 0)),
        ],
        out_specs=[
            pl.BlockSpec((nodes, units), lambda j: (j, 0)),
            pl.BlockSpec((nodes, LANES), lambda j: (0, j)),
        ],
        out_shape=[
            jax.ShapeDtypeStruct((FOUR * nodes, units), f32),
            jax.ShapeDtypeStruct((nodes, FOUR * LANES), bf16),
        ],
        scratch_shapes=[
            pltpu.VMEM((LANES, units), bf16),
            pltpu.VMEM((1, LANES), f32),
            pltpu.VMEM((LANES, nodes), f32),
        ],
        cost_estimate=pl.CostEstimate(
            flops=2 * FOUR * nodes * width * units, bytes_accessed=16 << 20, transcendentals=0
        ),
        name="forward",
    )(flat, w_in, b_in, wo_t, b_out, truth, area)


def cells_kernel(far_half, core_ref, cell_ref, pred_ref, out_ref):
    nodes = pred_ref.shape[0]
    half = core_ref[0] if not far_half else 1 - core_ref[0]
    ids = lax.broadcasted_iota(jnp.int32, (HALF, nodes), 0) + half * HALF
    picker = jnp.where(ids == cell_ref[...], 1.0, 0.0).astype(bf16)
    out_ref[...] = jnp.dot(picker, pred_ref[...], preferred_element_type=f32).astype(out_ref.dtype)


def cell_sums(core, cell, pred, far_half, dtype):
    return pl.pallas_call(
        functools.partial(cells_kernel, far_half),
        in_specs=[smem(), vmem(), vmem()],
        out_specs=vmem(),
        out_shape=jax.ShapeDtypeStruct((HALF, pred.shape[1]), dtype),
        compiler_params=fits(8),
        cost_estimate=pl.CostEstimate(
            flops=2 * HALF * pred.size, bytes_accessed=2 << 20, transcendentals=0
        ),
        name="cells",
    )(core, cell, pred)


def split_kernel(place_ref, pred_ref, *out_refs):
    for k, out_ref in enumerate(out_refs):
        out_ref[...] = pred_ref[(place_ref[0] + k) & 3]


def split(place, blocks):
    shape = jax.ShapeDtypeStruct(blocks.shape[1:], bf16)
    return pl.pallas_call(
        split_kernel,
        in_specs=[smem(), vmem()],
        out_specs=[vmem()] * FOUR,
        out_shape=[shape] * FOUR,
        compiler_params=fits(4),
        cost_estimate=pl.CostEstimate(flops=1 << 18, bytes_accessed=1 << 20, transcendentals=0),
        name="split",
    )(place, blocks)


def fine_kernel(place_ref, truth_ref, area_ref, *refs):
    got, grad, loss_ref, part, slope = refs[:4], refs[4:8], refs[8], refs[9], refs[10]
    for k in range(MEMBERS):
        block = got[k // FOUR][:, (k % FOUR) * LANES : (k % FOUR + 1) * LANES]
        part[k] = block.astype(f32).T[:VARS, :]
    start = pl.multiple_of(place_ref[0] * LANES, LANES)
    truth = truth_ref[:, pl.ds(start, LANES)]
    area = area_ref[:, pl.ds(start, LANES)]
    slope[:, VARS:, :] = jnp.zeros((MEMBERS, LANES - VARS, LANES), f32)

    def member(m, carry):
        truths, pairs = carry
        own = part[m]
        off = own - truth
        mean = jnp.sum(off * off, axis=0, keepdims=True) * (1.0 / VARS) + EPSILON
        inverse = lax.rsqrt(mean)
        truths = truths + mean * inverse
        total = jnp.zeros_like(own)
        for k in range(MEMBERS):
            between = own - part[k]
            mean = jnp.sum(between * between, axis=0, keepdims=True) * (1.0 / VARS) + EPSILON
            weight = lax.rsqrt(mean)
            distinct = jnp.where(m == k, 0.0, 1.0)
            pairs = pairs + (mean * weight) * distinct
            total = total + between * weight
        slope[m, :VARS, :] = off * (inverse * area * TRUTH_SCALE) - total * (area * PAIR_SCALE)
        return truths, pairs

    zero = jnp.zeros((1, LANES), f32)
    truths, pairs = lax.fori_loop(0, MEMBERS, member, (zero, zero))
    loss_ref[...] = area * (truths * (1.0 / MEMBERS) - pairs * (0.5 / PAIRS))
    for k in range(MEMBERS):
        grad[k // FOUR][:, (k % FOUR) * LANES : (k % FOUR + 1) * LANES] = slope[k].T.astype(bf16)


def fine(place, truth, area, got):
    shape = jax.ShapeDtypeStruct(got[0].shape, bf16)
    return pl.pallas_call(
        fine_kernel,
        in_specs=[smem()] + [vmem()] * 6,
        out_specs=[vmem()] * 5,
        out_shape=[shape] * FOUR + [jax.ShapeDtypeStruct((1, LANES), f32)],
        compiler_params=fits(10),
        scratch_shapes=[
            pltpu.VMEM((MEMBERS, VARS, LANES), f32),
            pltpu.VMEM((MEMBERS, LANES, LANES), f32),
        ],
        cost_estimate=pl.CostEstimate(
            flops=MEMBERS * MEMBERS * VARS * LANES * 16, bytes_accessed=2 << 20, transcendentals=0
        ),
        name="fine",
    )(place, truth, area, *got)


def three(value):
    high = value.astype(bf16).astype(f32)
    rest = value - high
    middle = rest.astype(bf16).astype(f32)
    return high, middle, rest - middle


def coarse_kernel(got_ref, loss_ref, area_ref, out_ref):
    places = got_ref.shape[0] // FOUR
    lane = lax.broadcasted_iota(jnp.int32, (8, LANES), 1)
    rank = lax.broadcasted_iota(jnp.int32, (8, LANES), 0)
    real = lane < VARS
    spare = lane >= VARS + 24
    sums = []
    for m in range(FOUR):
        total = got_ref[m].astype(f32)
        for s in range(1, places):
            total = total + got_ref[s * FOUR + m].astype(f32)
        sums += [total[:, j * LANES : (j + 1) * LANES] for j in range(FOUR)]

    def across(value):
        return jnp.sum(value, axis=1, keepdims=True)

    counts = across(jnp.where(spare, sums[0] + sums[1], 0.0))
    weight = across(jnp.where(spare, sums[2], 0.0))
    inverse = 1.0 / jnp.maximum(counts, 1.0)
    truth = jnp.zeros((8, LANES), f32)
    for j in range(FOUR):
        turned = pltpu.roll(sums[j], (24 * j - VARS) % LANES, 1)
        truth = jnp.where((lane >= 24 * j) & (lane < 24 * (j + 1)), turned, truth)
    truth = truth * inverse
    means = [jnp.where(real, (v * inverse).astype(bf16).astype(f32), 0.0) for v in sums]
    truths = jnp.zeros((8, 1), f32)
    pairs = jnp.zeros((8, 1), f32)
    grads = []
    for m in range(MEMBERS):
        off = means[m] - truth
        mean = across(off * off) * (1.0 / VARS) + EPSILON
        turn = lax.rsqrt(mean)
        truths = truths + mean * turn
        grads.append(off * (turn * TRUTH_SCALE))
    for m in range(MEMBERS):
        for k in range(m):
            between = means[m] - means[k]
            mean = across(between * between) * (1.0 / VARS) + EPSILON
            turn = lax.rsqrt(mean)
            pairs = pairs + mean * turn
            pull = between * (turn * PAIR_SCALE)
            grads[m] = grads[m] - pull
            grads[k] = grads[k] + pull
    loss = jnp.sum(weight * (truths * (1.0 / MEMBERS) - pairs * (1.0 / PAIRS)), axis=0, keepdims=True)
    fine_loss = across(loss_ref[...])
    area = across(area_ref[...])
    pieces = jnp.zeros((8, LANES), f32)
    for index, value in enumerate((*three(fine_loss), *three(loss), *three(area))):
        pieces = jnp.where(lane == VARS + index, value, pieces)
    pieces = jnp.where(rank == 0, pieces, 0.0)
    scale = weight * inverse
    for m in range(FOUR):
        rows = [grads[m * FOUR + j] * scale for j in range(FOUR)]
        rows[0] = rows[0] + pieces
        block = jnp.concatenate(rows, axis=1).astype(bf16)
        for s in range(places):
            out_ref[s * FOUR + m] = block


def coarse(got, loss, area):
    return pl.pallas_call(
        coarse_kernel,
        in_specs=[vmem(), vmem(), vmem()],
        out_specs=vmem(),
        out_shape=jax.ShapeDtypeStruct(got.shape, bf16),
        compiler_params=fits(6),
        cost_estimate=pl.CostEstimate(flops=1 << 21, bytes_accessed=1 << 20, transcendentals=0),
        name="coarse",
    )(got, loss, area)


def picked(half, column, table):
    first = (half * HALF).astype(f32)
    ids = lax.broadcasted_iota(jnp.int32, (column.shape[0], HALF), 1).astype(f32) + first
    wide = jnp.concatenate([column] * (HALF // LANES), axis=1)
    picker = jnp.where(ids == wide, 1.0, 0.0).astype(bf16)
    return jnp.dot(picker, table, preferred_element_type=f32)


def base_kernel(place_ref, cell_ref, *refs):
    got, base_ref, column_ref = refs[:4], refs[4], refs[5]
    nodes = cell_ref.shape[1]
    column_ref[...] = jnp.broadcast_to(cell_ref[...].astype(f32), (LANES, nodes)).T
    for k in range(FOUR):
        base_ref[(place_ref[0] + k) & 3] = got[k][...].astype(f32)


def based(place, cell, got):
    return pl.pallas_call(
        base_kernel,
        in_specs=[smem()] + [vmem()] * 5,
        out_specs=[vmem(), vmem()],
        out_shape=[
            jax.ShapeDtypeStruct((FOUR, *got[0].shape), f32),
            jax.ShapeDtypeStruct((cell.shape[1], LANES), f32),
        ],
        compiler_params=fits(6),
        cost_estimate=pl.CostEstimate(flops=1 << 20, bytes_accessed=2 << 20, transcendentals=0),
        name="base",
    )(place, cell, *got)


def near_kernel(core_ref, column_ref, base_ref, table_ref, out_ref):
    out_ref[...] = base_ref[...] + picked(core_ref[0], column_ref[...], table_ref[...])


def near(core, column, base, table):
    return pl.pallas_call(
        near_kernel,
        in_specs=[smem(), vmem(), vmem(), vmem()],
        out_specs=vmem(),
        out_shape=jax.ShapeDtypeStruct(base.shape, f32),
        compiler_params=fits(8),
        cost_estimate=pl.CostEstimate(
            flops=2 * HALF * table.size, bytes_accessed=2 << 20, transcendentals=0
        ),
        name="near",
    )(core, column, base, table)


def far_kernel(
    core_ref, column_ref, near_ref, own_ref, other_ref, up_ref, factor_ref, score_ref
):
    total = near_ref[...] + picked(1 - core_ref[0], column_ref[...], other_ref[...])
    up_ref[...] = total.astype(bf16)
    sums = own_ref[:, :LANES].astype(f32) + other_ref[:, :LANES].astype(f32)
    sums = jnp.sum(sums, axis=0, keepdims=True)
    lane = lax.broadcasted_iota(jnp.int32, (1, LANES), 1)

    def of(index):
        here = (lane >= VARS + 3 * index) & (lane < VARS + 3 * index + 3)
        return jnp.sum(jnp.where(here, sums, 0.0), axis=1, keepdims=True)

    area = of(2) * (1.0 / FOUR)
    factor_ref[...] = jnp.broadcast_to(LOSS_SCALE * NODE_TOTAL / area, (1, LANES))
    score_ref[0] = (of(0) / area)[0, 0]
    score_ref[1] = (of(1) / area)[0, 0]


def far(core, column, near_part, own, other):
    return pl.pallas_call(
        far_kernel,
        in_specs=[smem()] + [vmem()] * 4,
        out_specs=[vmem(), vmem(), smem()],
        compiler_params=fits(10),
        out_shape=[
            jax.ShapeDtypeStruct(near_part.shape, bf16),
            jax.ShapeDtypeStruct((1, LANES), f32),
            jax.ShapeDtypeStruct((2,), f32),
        ],
        name="far",
    )(core, column, near_part, own, other)


def backward_kernel(up_ref, preact_ref, wo_ref, w_ref, factor_ref, out_ref, wide, grads):
    @pl.when(pl.program_id(0) == 0)
    def _():
        wide[:VARS, :] = wo_ref[...]
        wide[VARS:, :] = jnp.zeros((LANES - VARS, wide.shape[1]), bf16)

    units = w_ref.shape[1]
    step = 256
    for n in range(0, units, step):
        hidden = jnp.dot(up_ref[...], wide[:, n : n + step], preferred_element_type=f32)
        pre = preact_ref[:, n : n + step]
        sigma = 0.5 * jnp.tanh(0.5 * pre) + 0.5
        slope = sigma * (1.0 + pre * (1.0 - sigma))
        grads[:, n : n + step] = (hidden * slope).astype(bf16)
    for n in range(0, w_ref.shape[0], step):
        total = lax.dot_general(
            grads[...], w_ref[n : n + step, :], (((1,), (1,)), ((), ())), preferred_element_type=f32
        )
        out_ref[:, n : n + step] = (total * factor_ref[0:1, 0:1]).astype(bf16)


def backward(up, preact, wo_t, w_in, factor, nodes):
    width, units = w_in.shape
    return pl.pallas_call(
        backward_kernel,
        grid=(FOUR,),
        in_specs=[
            pl.BlockSpec((nodes, LANES), lambda j: (0, j)),
            pl.BlockSpec((nodes, units), lambda j: (j, 0)),
            pl.BlockSpec((VARS, units), lambda j: (0, 0)),
            pl.BlockSpec((width, units), lambda j: (0, 0)),
            pl.BlockSpec((1, LANES), lambda j: (0, 0)),
        ],
        out_specs=pl.BlockSpec((nodes, width), lambda j: (j, 0)),
        out_shape=jax.ShapeDtypeStruct((FOUR * nodes, width), bf16),
        scratch_shapes=[pltpu.VMEM((LANES, units), bf16), pltpu.VMEM((nodes, units), bf16)],
        cost_estimate=pl.CostEstimate(
            flops=2 * FOUR * nodes * width * units, bytes_accessed=16 << 20, transcendentals=0
        ),
        name="backward",
    )(up, preact, wo_t, w_in, factor)


def turned(block, places):
    return lax.ppermute(block, "m", [(j, (j + places) % FOUR) for j in range(FOUR)])


def shards(latent, w_in, b_in, w_out, b_out, target, area, cell_of):
    members, nodes, width = latent.shape
    flat = latent.reshape(members * nodes, width)
    wo_t = w_out.T
    truth = target.T
    cell = cell_of[None, :]
    area_row = area[None, :]
    place = lax.axis_index("m").astype(jnp.int32)[None]
    core = lax.axis_index("c").astype(jnp.int32)[None]
    swap = [(0, 1), (1, 0)]

    preact, pred = forward(flat, w_in, b_in[None, :], wo_t, b_out[None, :], truth, area_row, nodes)
    sent = cell_sums(core, cell, pred, True, bf16)
    arrived = lax.ppermute(sent, "c", swap)
    blocks = split(place, pred.reshape(FOUR, LANES, FOUR * LANES))
    parts = [blocks[0]] + [turned(blocks[k], k) for k in range(1, FOUR)]
    kept = cell_sums(core, cell, pred, False, f32)
    both = (kept + arrived.astype(f32)).astype(bf16).reshape(64, 8, FOUR * LANES)
    gathered = lax.all_to_all(both, WIDE, 0, 0, tiled=True)
    *grads, fine_loss = fine(place, truth, area_row, parts)
    grads = [grads[0]] + [turned(grads[k], -k) for k in range(1, FOUR)]
    table = coarse(gathered, fine_loss, area_row)
    own = lax.all_to_all(table, WIDE, 0, 0, tiled=True)
    own = own.reshape(HALF, FOUR * LANES)
    base, column = based(place, cell, grads)
    other = lax.ppermute(own, "c", swap)
    near_part = near(core, column, base.reshape(nodes, FOUR * LANES), own)
    up, factor, scores = far(core, column, near_part, own, other)
    latent_grad = backward(up, preact, wo_t, w_in, factor, nodes)
    return (latent_grad.reshape(members, nodes, width), scores)


def solution(mesh):
    split = Mesh(mesh.devices.reshape(4, 4, 2, mesh.shape["member"]), ("x", "y", "c", "m"))
    return jax.shard_map(
        shards,
        mesh=split,
        in_specs=(P("m", SPACE, None), P(), P(), P(), P(), P(SPACE, None), P(SPACE), P(SPACE)),
        out_specs=(P("m", SPACE, None), P()),
        check_vma=False,
    )
```

time: 116 us -> 92.3 us (0.80)
  Pallas kernels: 47.3 us -> 26.5 us
  local copies, waits for them, and re-layouts: 9.02 us -> 2.49 us
  blocking collectives: 16.8 us -> 20.8 us
  other arithmetic: 4.5 us -> 1.01 us
  starting transfers between devices: 17.4 us -> 20.2 us
    pallas_call x7 -> x9, Pallas kernels: 45 us -> 26.1 us  [the longest x1 10.4 us: backward(): pl.pallas_call(backward_kernel, grid=(FOUR,), in_specs=[pl.BlockSpec((nod...]
    ppermute x0 -> x6, waiting for transfers between devices: none -> 17.8 us  [turned(): lax.ppermute(block, 'm', [(j, (j + places) % FOUR) for j in range(FOUR)])]
    all_to_all x2 -> x0, waiting for transfers between devices: 11.7 us -> none  [the longest x1 6.29 us: shards(): lax.all_to_all(fine_grad, 'm', 0, 0, tiled=True)]
    all_to_all x2 -> x0, starting transfers between devices: 8.9 us -> none  [the longest x1 5.43 us: shards(): lax.all_to_all(pred.reshape(FOUR, LANES, FOUR * LANES), 'm', 0, 0, tiled=...]
    ppermute x0 -> x6, starting transfers between devices: none -> 8.55 us  [turned(): lax.ppermute(block, 'm', [(j, (j + places) % FOUR) for j in range(FOUR)])]
    all_to_all x1, waiting for transfers between devices: 7.38 us -> 0.01 us  [shards(): gathered = lax.all_to_all(both, WIDE, 0, 0, tiled=True)]
    all_to_all x1, blocking collectives: 16.8 us -> 20.8 us  [shards(): own = lax.all_to_all(table, WIDE, 0, 0, tiled=True)]
    all_to_all x1, starting transfers between devices: 8.54 us -> 11.5 us  [shards(): gathered = lax.all_to_all(both, WIDE, 0, 0, tiled=True)]
  transfers between devices with their start and end apart: 5 -> 9, of which waited for: 3 -> 6; matrix products, arithmetic and copies ran while one was open for 3% -> 0% of each run, Pallas kernels for 9% -> 5%
where the time goes in v2:
time: 92.3 us; the launch traced here: 91 us
  Pallas kernels  26.5 us (29%)
  blocking collectives  20.8 us (23%)
  starting transfers between devices  20.2 us (22%)
  waiting for transfers between devices  19.2 us (21%)
  local copies, waits for them, and re-layouts  2.49 us (3%)
  other arithmetic  1.01 us (1%)
    all_to_all x1, blocking collectives, shards(): own = lax.all_to_all(table, WIDE, 0, 0, tiled=True)  20.8 us
    ppermute x6, waiting for transfers between devices, turned(): lax.ppermute(block, 'm', [(j, (j + places) % FOUR) for j in range(FOUR)])  17.8 us
    all_to_all x1, starting transfers between devices, shards(): gathered = lax.all_to_all(both, WIDE, 0, 0, tiled=True)  11.5 us
    pallas_call x1, Pallas kernels, backward(): pl.pallas_call(backward_kernel, grid=(FOUR,), in_specs=[pl.BlockSpec((nod...  10.4 us
    pallas_call x1, Pallas kernels, forward(): pl.pallas_call(forward_kernel, grid=(FOUR,), in_specs=[pl.BlockSpec((node...  10.1 us
    ppermute x6, starting transfers between devices, turned(): lax.ppermute(block, 'm', [(j, (j + places) % FOUR) for j in range(FOUR)])  8.55 us
    pallas_call x1, Pallas kernels, fine(): pl.pallas_call(fine_kernel, in_specs=[smem()] + [vmem()] * 6, out_specs=[...  3.24 us
    unnamed x14, local copies, waits for them, and re-layouts  2.49 us
  transfers between devices with their start and end apart: 9, of which 6 were waited for; matrix products, arithmetic and copies ran while one was open for 0% of the time, Pallas kernels for 5%

profile of v2, /device:TPU:0, one launch (start us, length us, event | category | flops | bytes accessed | tf_op | source)
XLA Modules:
  0.0 91.0 jit_solution(2868650380011048031)
XLA Ops:
  0.7 10.1 %forward.1 = (f32[2048,1024]{1,0:T(8,128)}, bf16[512,512]{1,0:T(8,128)(2,1)}) custom-call(bf16[2048,1024]{1,0:T(8,128)(2,1)} %bitcast.28, bf16[1024,1024]{1,0:T(8,128)(2,1)} %w_ref.3, f32[1,1024]{1,0:T(1,128)} %bitcast.31, bf16[96,1024]{1,0:T(8,128)(2,1)} %bitcast.29, f32[1,96]{1,0:T(1,128)} %bitcast.32, f32[96,512]{1,0:T(8,128)} %bitcast.20, f32[1,512]{1,0:T(1,128)} %bitcast.25), custom_call_target="tpu_custom_call" | custom-call | flops 4294967296 | bytes 16777216 | tf_op jit(solution)/shard_map/forward/pallas_call | solution.py:74
  10.7 0.0 copy-start
  10.8 1.0 %copy-done = bf16[512,512]{1,0:T(8,128)(2,1)S(1)} copy-done((bf16[512,512]{1,0:T(8,128)(2,1)S(1)}, bf16[512,512]{1,0:T(8,128)(2,1)}, u32[]{:S(2)}) %copy-start) | copy-done | bytes 524312
  11.8 0.4 cells.3
  12.2 0.1 collective-permute-start.6
  12.3 0.4 cells.2
  12.8 1.5 %collective-permute-done.6 = bf16[512,512]{1,0:T(8,128)(2,1)S(1)} collective-permute-done((bf16[512,512]{1,0:T(8,128)(2,1)S(1)}, bf16[512,512]{1,0:T(8,128)(2,1)S(1)}, u32[]{:S(2)}, u32[]{:S(2)}) %collective-permute-start.6) | collective-permute-done | bytes 524320 | tf_op jit(solution)/shard_map/ppermute | solution.py:421
  14.2 1.0 %fusion = bf16[64,8,512]{2,1,0:T(8,128)(2,1)} fusion(f32[512,512]{1,0:T(8,128)S(1)} %cells.2, bf16[512,512]{1,0:T(8,128)(2,1)S(1)} %collective-permute-done.6), kind=kLoop, calls=%fused_computation.1 | loop fusion | flops 786432 | bytes 2097152 | tf_op jit(solution)/shard_map/reshape | solution.py:425
  15.2 11.5 %all-to-all-start = ((bf16[64,8,512]{2,1,0:T(8,128)(2,1)}), bf16[64,8,512]{2,1,0:T(8,128)(2,1)S(1)}, u32[]{:S(2)}, u32[]{:S(2)}) async-start(bf16[64,8,512]{2,1,0:T(8,128)(2,1)} %fusion), calls=%async_computation | async-start | bytes 1048576 | tf_op jit(solution)/shard_map/all_to_all | solution.py:426
  26.8 1.6 %collective-permute-start = (bf16[128,512]{1,0:T(8,128)(2,1)S(1)}, bf16[128,512]{1,0:T(8,128)(2,1)S(1)}, u32[]{:S(2)}, u32[]{:S(2)}) collective-permute-start(bf16[128,512]{1,0:T(8,128)(2,1)S(1)} %get-tuple-element.20), channel_id=1, source_target_pairs={{0,1},{1,2},{2,3},{3,0},{4,5},{5,6},{6,7},{7,4},{8,9},{9,10},{10,1... | collective-permute-start | bytes 393224 | tf_op jit(solution)/shard_map/ppermute | solution.py:405
  28.5 2.7 %collective-permute-start.1 = (bf16[128,512]{1,0:T(8,128)(2,1)S(1)}, bf16[128,512]{1,0:T(8,128)(2,1)S(1)}, u32[]{:S(2)}, u32[]{:S(2)}) collective-permute-start(bf16[128,512]{1,0:T(8,128)(2,1)S(1)} %get-tuple-element.21), channel_id=1, source_target_pairs={{0,2},{1,3},{2,0},{3,1},{4,6},{5,7},{6,4},{7,5},{8,10},{9,11},{10,... | collective-permute-start | bytes 393224 | tf_op jit(solution)/shard_map/ppermute | solution.py:405
  31.2 1.5 %collective-permute-start.2 = (bf16[128,512]{1,0:T(8,128)(2,1)S(1)}, bf16[128,512]{1,0:T(8,128)(2,1)S(1)}, u32[]{:S(2)}, u32[]{:S(2)}) collective-permute-start(bf16[128,512]{1,0:T(8,128)(2,1)S(1)} %get-tuple-element.22), channel_id=1, source_target_pairs={{0,3},{1,0},{2,1},{3,2},{4,7},{5,4},{6,5},{7,6},{8,11},{9,8},{10,9... | collective-permute-start | bytes 393224 | tf_op jit(solution)/shard_map/ppermute | solution.py:405
  32.6 5.7 %collective-permute-done.refs_1_ = bf16[128,512]{1,0:T(8,128)(2,1)S(1)} collective-permute-done((bf16[128,512]{1,0:T(8,128)(2,1)S(1)}, bf16[128,512]{1,0:T(8,128)(2,1)S(1)}, u32[]{:S(2)}, u32[]{:S(2)}) %collective-permute-start) | collective-permute-done | bytes 131104 | tf_op jit(solution)/shard_map/ppermute | solution.py:405
  38.3 3.9 %collective-permute-done.1.refs_2_ = bf16[128,512]{1,0:T(8,128)(2,1)S(1)} collective-permute-done((bf16[128,512]{1,0:T(8,128)(2,1)S(1)}, bf16[128,512]{1,0:T(8,128)(2,1)S(1)}, u32[]{:S(2)}, u32[]{:S(2)}) %collective-permute-start.1) | collective-permute-done | bytes 131104 | tf_op jit(solution)/shard_map/ppermute | solution.py:405
  42.3 0.0 collective-permute-done.2.refs_3_
  42.3 3.2 %fine.1 = (bf16[128,512]{1,0:T(8,128)(2,1)S(1)}, bf16[128,512]{1,0:T(8,128)(2,1)S(1)}, bf16[128,512]{1,0:T(8,128)(2,1)S(1)}, bf16[128,512]{1,0:T(8,128)(2,1)S(1)}, f32[1,128]{1,0:T(1,128)S(1)}) custom-call(s32[1]{0:T(128)} %bitcast.1.place_ref, f32[96,512]{1,0:T(8,128)S(1)} %bitcast.21, f32[1,512]{1,0:T(1,128)S(1)} %bitcast.26, ...), custom_call_target="tpu_custom_call" | custom-call | flops 50331648 | bytes 2097152 | tf_op jit(solution)/shard_map/fine/pallas_call | solution.py:183
  45.5 0.0 all-to-all-done.got_ref
  45.5 0.4 coarse.1
  46.0 20.8 %all_to_all.10 = bf16[64,8,512]{2,1,0:T(8,128)(2,1)S(1)} all-to-all(bf16[64,8,512]{2,1,0:T(8,128)(2,1)S(1)} %coarse.1), channel_id=1, replica_groups=mesh['x'=4,'y'=4,'c'=2,'m'=4] {'x','y','m'}, dimensions={0} | all-to-all | bytes 1048576 | tf_op jit(solution)/shard_map/all_to_all | solution.py:430
  66.7 0.0 collective-permute-start.7
  66.7 1.0 %collective-permute-start.3 = (bf16[128,512]{1,0:T(8,128)(2,1)S(1)}, bf16[128,512]{1,0:T(8,128)(2,1)S(1)}, u32[]{:S(2)}, u32[]{:S(2)}) collective-permute-start(bf16[128,512]{1,0:T(8,128)(2,1)S(1)} %get-tuple-element.24), channel_id=1, source_target_pairs={{0,3},{1,0},{2,1},{3,2},{4,7},{5,4},{6,5},{7,6},{8,11},{9,8},{10,9... | collective-permute-start | bytes 393224 | tf_op jit(solution)/shard_map/ppermute | solution.py:405
  67.7 1.7 %collective-permute-start.4 = (bf16[128,512]{1,0:T(8,128)(2,1)S(1)}, bf16[128,512]{1,0:T(8,128)(2,1)S(1)}, u32[]{:S(2)}, u32[]{:S(2)}) collective-permute-start(bf16[128,512]{1,0:T(8,128)(2,1)S(1)} %get-tuple-element.25), channel_id=1, source_target_pairs={{0,2},{1,3},{2,0},{3,1},{4,6},{5,7},{6,4},{7,5},{8,10},{9,11},{10,... | collective-permute-start | bytes 393224 | tf_op jit(solution)/shard_map/ppermute | solution.py:405
  69.5 0.1 collective-permute-start.5
  69.5 3.6 %collective-permute-done.3.refs_1_ = bf16[128,512]{1,0:T(8,128)(2,1)S(1)} collective-permute-done((bf16[128,512]{1,0:T(8,128)(2,1)S(1)}, bf16[128,512]{1,0:T(8,128)(2,1)S(1)}, u32[]{:S(2)}, u32[]{:S(2)}) %collective-permute-start.3) | collective-permute-done | bytes 131104 | tf_op jit(solution)/shard_map/ppermute | solution.py:405
  73.1 2.5 %collective-permute-done.4.refs_2_ = bf16[128,512]{1,0:T(8,128)(2,1)S(1)} collective-permute-done((bf16[128,512]{1,0:T(8,128)(2,1)S(1)}, bf16[128,512]{1,0:T(8,128)(2,1)S(1)}, u32[]{:S(2)}, u32[]{:S(2)}) %collective-permute-start.4) | collective-permute-done | bytes 131104 | tf_op jit(solution)/shard_map/ppermute | solution.py:405
  75.6 2.1 %collective-permute-done.5.refs_3_ = bf16[128,512]{1,0:T(8,128)(2,1)S(1)} collective-permute-done((bf16[128,512]{1,0:T(8,128)(2,1)S(1)}, bf16[128,512]{1,0:T(8,128)(2,1)S(1)}, u32[]{:S(2)}, u32[]{:S(2)}) %collective-permute-start.5) | collective-permute-done | bytes 131104 | tf_op jit(solution)/shard_map/ppermute | solution.py:405
  77.7 0.1 base.1
  77.8 0.4 near.1.near_ref
  78.3 0.9 far.1
  79.2 0.8 copy-done.5
  80.0 0.6 copy-done.6
  80.6 10.4 %backward.1 = bf16[2048,1024]{1,0:T(8,128)(2,1)} custom-call(bf16[512,512]{1,0:T(8,128)(2,1)} %copy-done.5, f32[2048,1024]{1,0:T(8,128)} %get-tuple-element.31.preact_ref, bf16[96,1024]{1,0:T(8,128)(2,1)} %bitcast.30, bf16[1024,1024]{1,0:T(8,128)(2,1)} %w_ref.3, f32[1,128]{1,0:T(1,128)} %copy-done.6), custom_call_target="tpu_custom_call" | custom-call | flops 4294967296 | bytes 16777216 | tf_op jit(solution)/shard_map/backward/pallas_call | solution.py:384
  (12 shorter events, 0.1 us)
Async XLA Ops:
  0.6 10.1 %copy-start.3 = (s32[512]{0:T(512)S(1)}, s32[512]{0:T(512)}, u32[]{:S(2)}) copy-start(s32[512]{0:T(512)} %param.15) | copy-start | bytes 6148
  0.6 41.6 %copy-start.2 = (f32[512,96]{0,1:T(8,128)S(1)}, f32[512,96]{0,1:T(8,128)}, u32[]{:S(2)}) copy-start(f32[512,96]{0,1:T(8,128)} %param.13) | copy-start | bytes 589828
  10.7 31.5 %copy-start.4 = (f32[512]{0:T(512)S(1)}, f32[512]{0:T(512)}, u32[]{:S(2)}) copy-start(f32[512]{0:T(512)} %param.14) | copy-start | bytes 6148
  10.7 1.1 %copy-start = (bf16[512,512]{1,0:T(8,128)(2,1)S(1)}, bf16[512,512]{1,0:T(8,128)(2,1)}, u32[]{:S(2)}) copy-start(bf16[512,512]{1,0:T(8,128)(2,1)} %get-tuple-element.18.pred_ref) | copy-start | bytes 1572868
  11.8 15.0 %copy-start.1 = (bf16[512,512]{1,0:T(8,128)(2,1)S(1)}, bf16[512,512]{1,0:T(8,128)(2,1)}, u32[]{:S(2)}) copy-start(bf16[512,512]{1,0:T(8,128)(2,1)} %get-tuple-element.18.pred_ref) | copy-start | bytes 1572868
  12.2 2.0 %collective-permute-start.6 = (bf16[512,512]{1,0:T(8,128)(2,1)S(1)}, bf16[512,512]{1,0:T(8,128)(2,1)S(1)}, u32[]{:S(2)}, u32[]{:S(2)}) collective-permute-start(bf16[512,512]{1,0:T(8,128)(2,1)S(1)} %cells.3), channel_id=1, source_target_pairs={{0,4},{4,0},{1,5},{5,1},{2,6},{6,2},{3,7},{7,3},{8,12},{12,8},{9,1... | collective-permute-start | bytes 1572872 | tf_op jit(solution)/shard_map/ppermute | solution.py:421
  15.2 30.3 %all-to-all-start = ((bf16[64,8,512]{2,1,0:T(8,128)(2,1)}), bf16[64,8,512]{2,1,0:T(8,128)(2,1)S(1)}, u32[]{:S(2)}, u32[]{:S(2)}) async-start(bf16[64,8,512]{2,1,0:T(8,128)(2,1)} %fusion), calls=%async_computation | async-start | bytes 1048576 | tf_op jit(solution)/shard_map/all_to_all | solution.py:426
  26.8 11.5 %collective-permute-start = (bf16[128,512]{1,0:T(8,128)(2,1)S(1)}, bf16[128,512]{1,0:T(8,128)(2,1)S(1)}, u32[]{:S(2)}, u32[]{:S(2)}) collective-permute-start(bf16[128,512]{1,0:T(8,128)(2,1)S(1)} %get-tuple-element.20), channel_id=1, source_target_pairs={{0,1},{1,2},{2,3},{3,0},{4,5},{5,6},{6,7},{7,4},{8,9},{9,10},{10,1... | collective-permute-start | bytes 393224 | tf_op jit(solution)/shard_map/ppermute | solution.py:405
  28.5 13.8 %collective-permute-start.1 = (bf16[128,512]{1,0:T(8,128)(2,1)S(1)}, bf16[128,512]{1,0:T(8,128)(2,1)S(1)}, u32[]{:S(2)}, u32[]{:S(2)}) collective-permute-start(bf16[128,512]{1,0:T(8,128)(2,1)S(1)} %get-tuple-element.21), channel_id=1, source_target_pairs={{0,2},{1,3},{2,0},{3,1},{4,6},{5,7},{6,4},{7,5},{8,10},{9,11},{10,... | collective-permute-start | bytes 393224 | tf_op jit(solution)/shard_map/ppermute | solution.py:405
  31.2 11.1 %collective-permute-start.2 = (bf16[128,512]{1,0:T(8,128)(2,1)S(1)}, bf16[128,512]{1,0:T(8,128)(2,1)S(1)}, u32[]{:S(2)}, u32[]{:S(2)}) collective-permute-start(bf16[128,512]{1,0:T(8,128)(2,1)S(1)} %get-tuple-element.22), channel_id=1, source_target_pairs={{0,3},{1,0},{2,1},{3,2},{4,7},{5,4},{6,5},{7,6},{8,11},{9,8},{10,9... | collective-permute-start | bytes 393224 | tf_op jit(solution)/shard_map/ppermute | solution.py:405
  66.7 11.5 %collective-permute-start.7 = (bf16[512,512]{1,0:T(8,128)(2,1)S(1)}, bf16[512,512]{1,0:T(8,128)(2,1)S(1)}, u32[]{:S(2)}, u32[]{:S(2)}) collective-permute-start(bf16[512,512]{1,0:T(8,128)(2,1)S(1)} %bitcast.16), channel_id=1, source_target_pairs={{0,4},{4,0},{1,5},{5,1},{2,6},{6,2},{3,7},{7,3},{8,12},{12,8},{9,1... | collective-permute-start | bytes 1572872 | tf_op jit(solution)/shard_map/ppermute | solution.py:433
  66.7 6.4 %collective-permute-start.3 = (bf16[128,512]{1,0:T(8,128)(2,1)S(1)}, bf16[128,512]{1,0:T(8,128)(2,1)S(1)}, u32[]{:S(2)}, u32[]{:S(2)}) collective-permute-start(bf16[128,512]{1,0:T(8,128)(2,1)S(1)} %get-tuple-element.24), channel_id=1, source_target_pairs={{0,3},{1,0},{2,1},{3,2},{4,7},{5,4},{6,5},{7,6},{8,11},{9,8},{10,9... | collective-permute-start | bytes 393224 | tf_op jit(solution)/shard_map/ppermute | solution.py:405
  67.7 7.9 %collective-permute-start.4 = (bf16[128,512]{1,0:T(8,128)(2,1)S(1)}, bf16[128,512]{1,0:T(8,128)(2,1)S(1)}, u32[]{:S(2)}, u32[]{:S(2)}) collective-permute-start(bf16[128,512]{1,0:T(8,128)(2,1)S(1)} %get-tuple-element.25), channel_id=1, source_target_pairs={{0,2},{1,3},{2,0},{3,1},{4,6},{5,7},{6,4},{7,5},{8,10},{9,11},{10,... | collective-permute-start | bytes 393224 | tf_op jit(solution)/shard_map/ppermute | solution.py:405
  69.5 8.2 %collective-permute-start.5 = (bf16[128,512]{1,0:T(8,128)(2,1)S(1)}, bf16[128,512]{1,0:T(8,128)(2,1)S(1)}, u32[]{:S(2)}, u32[]{:S(2)}) collective-permute-start(bf16[128,512]{1,0:T(8,128)(2,1)S(1)} %get-tuple-element.26), channel_id=1, source_target_pairs={{0,1},{1,2},{2,3},{3,0},{4,5},{5,6},{6,7},{7,4},{8,9},{9,10},{10,1... | collective-permute-start | bytes 393224 | tf_op jit(solution)/shard_map/ppermute | solution.py:405
  79.2 0.9 copy-start.5
  80.0 0.6 copy-start.6

commit v3 on v2

--- a/solution.py
+++ b/solution.py
@@ -1,5 +1,3 @@
-import functools
-
 import jax
 import jax.numpy as jnp
 from jax import lax
@@ -36,12 +34,16 @@
     return pltpu.CompilerParams(vmem_limit_bytes=mib << 20)
 
 
+def in_hbm(value):
+    return pltpu.with_memory_space_constraint(value, pltpu.HBM)
+
+
 def smem():
     return pl.BlockSpec(memory_space=pltpu.SMEM)
 
 
 def forward_kernel(
-    x_ref, w_ref, b_ref, wo_ref, bo_ref, truth_ref, area_ref, preact_ref, pred_ref, wide, bias, extra
+    x_ref, w_ref, b_ref, wo_ref, bo_ref, truth_ref, area_ref, cell_ref, slope_ref, pred_ref, wide, bias, extra
 ):
     j = pl.program_id(0)
     nodes = x_ref.shape[0]
@@ -59,17 +61,21 @@
     rank = lax.broadcasted_iota(jnp.int32, (8, nodes), 0)
     ones = jnp.where((lane & 15) == rank + 8 * j, 1.0, 0.0)
     spread = jnp.where((lane & 7) == rank, area_ref[...], 0.0)
+    high, low = cell_ref[...] >> 5, cell_ref[...] & 31
+    ids = jnp.where(rank == 0, high, jnp.where(rank == 1, low, 0)).astype(f32)
+    features = jnp.where(j < 2, ones, jnp.where(j == 2, spread, ids))
     extra[VARS : VARS + 24, :] = truth_ref[pl.ds(pl.multiple_of(24 * j, 8), 24), :]
-    extra[VARS + 24 :, :] = jnp.where(j < 2, ones, jnp.where(j == 2, spread, 0.0))
+    extra[VARS + 24 :, :] = features
     pre = jnp.dot(x_ref[...], w_ref[...], preferred_element_type=f32) + b_ref[...]
-    preact_ref[...] = pre
-    half = 0.5 * pre
-    act = (half + half * jnp.tanh(half)).astype(bf16)
+    sigma = 0.5 * jnp.tanh(0.5 * pre) + 0.5
+    silu = pre * sigma
+    slope_ref[...] = (sigma + silu * (1.0 - sigma)).astype(bf16)
+    act = silu.astype(bf16)
     total = lax.dot_general(act, wide[...], (((1,), (1,)), ((), ())), preferred_element_type=f32)
     pred_ref[...] = (total + bias[...] + extra[...].T).astype(bf16)
 
 
-def forward(flat, w_in, b_in, wo_t, b_out, truth, area, nodes):
+def forward(flat, w_in, b_in, wo_t, b_out, truth, area, cell, nodes):
     width, units = w_in.shape
     return pl.pallas_call(
         forward_kernel,
@@ -82,13 +88,14 @@
             pl.BlockSpec((1, VARS), lambda j: (0, 0)),
             pl.BlockSpec((VARS, nodes), lambda j: (0, 0)),
             pl.BlockSpec((1, nodes), lambda j: (0, 0)),
+            pl.BlockSpec((1, nodes), lambda j: (0, 0)),
         ],
         out_specs=[
             pl.BlockSpec((nodes, units), lambda j: (j, 0)),
             pl.BlockSpec((nodes, LANES), lambda j: (0, j)),
         ],
         out_shape=[
-            jax.ShapeDtypeStruct((FOUR * nodes, units), f32),
+            pltpu.HBM((FOUR * nodes, units), bf16),
             jax.ShapeDtypeStruct((nodes, FOUR * LANES), bf16),
         ],
         scratch_shapes=[
@@ -96,33 +103,60 @@
             pltpu.VMEM((1, LANES), f32),
             pltpu.VMEM((LANES, nodes), f32),
         ],
+        compiler_params=fits(24),
         cost_estimate=pl.CostEstimate(
             flops=2 * FOUR * nodes * width * units, bytes_accessed=16 << 20, transcendentals=0
         ),
         name="forward",
-    )(flat, w_in, b_in, wo_t, b_out, truth, area)
-
-
-def cells_kernel(far_half, core_ref, cell_ref, pred_ref, out_ref):
-    nodes = pred_ref.shape[0]
-    half = core_ref[0] if not far_half else 1 - core_ref[0]
-    ids = lax.broadcasted_iota(jnp.int32, (HALF, nodes), 0) + half * HALF
-    picker = jnp.where(ids == cell_ref[...], 1.0, 0.0).astype(bf16)
-    out_ref[...] = jnp.dot(picker, pred_ref[...], preferred_element_type=f32).astype(out_ref.dtype)
-
-
-def cell_sums(core, cell, pred, far_half, dtype):
-    return pl.pallas_call(
-        functools.partial(cells_kernel, far_half),
+    )(flat, w_in, b_in, wo_t, b_out, truth, area, cell)
+
+
+def gathered_rows(core, ids, pred):
+    here = lax.broadcasted_iota(jnp.int32, (HALF, pred.shape[0]), 0) + core * HALF
+    picker = jnp.where(here == ids, 1.0, 0.0).astype(bf16)
+    return jnp.dot(picker, pred, preferred_element_type=f32)
+
+
+def ours_kernel(core_ref, cell_ref, pred_ref, out_ref):
+    out_ref[...] = gathered_rows(core_ref[0], cell_ref[...], pred_ref[...])
+
+
+def ours(core, cell, pred):
+    return pl.pallas_call(
+        ours_kernel,
         in_specs=[smem(), vmem(), vmem()],
         out_specs=vmem(),
-        out_shape=jax.ShapeDtypeStruct((HALF, pred.shape[1]), dtype),
+        out_shape=jax.ShapeDtypeStruct((HALF, pred.shape[1]), f32),
         compiler_params=fits(8),
         cost_estimate=pl.CostEstimate(
             flops=2 * HALF * pred.size, bytes_accessed=2 << 20, transcendentals=0
         ),
-        name="cells",
+        name="ours",
     )(core, cell, pred)
+
+
+def theirs_kernel(core_ref, ours_ref, pred_ref, out_ref):
+    lane = lax.broadcasted_iota(jnp.int32, (8, LANES), 1)
+    digits = jnp.where(lane == VARS + 24, 32.0, jnp.where(lane == VARS + 25, 1.0, 0.0)).astype(bf16)
+    last = pred_ref[:, (FOUR - 1) * LANES :]
+    ids = lax.dot_general(digits, last, (((1,), (1,)), ((), ())), preferred_element_type=f32)
+    ids = ids[0:1, :].astype(jnp.int32)
+    total = ours_ref[...] + gathered_rows(core_ref[0], ids, pred_ref[...])
+    out_ref[...] = total.astype(bf16)
+
+
+def theirs(core, partial, pred):
+    return pl.pallas_call(
+        theirs_kernel,
+        in_specs=[smem(), vmem(), vmem()],
+        out_specs=vmem(),
+        out_shape=jax.ShapeDtypeStruct(partial.shape, bf16),
+        compiler_params=fits(8),
+        cost_estimate=pl.CostEstimate(
+            flops=2 * HALF * pred.size, bytes_accessed=2 << 20, transcendentals=0
+        ),
+        name="theirs",
+    )(core, partial, pred)
 
 
 def split_kernel(place_ref, pred_ref, *out_refs):
@@ -151,31 +185,37 @@
     start = pl.multiple_of(place_ref[0] * LANES, LANES)
     truth = truth_ref[:, pl.ds(start, LANES)]
     area = area_ref[:, pl.ds(start, LANES)]
-    slope[:, VARS:, :] = jnp.zeros((MEMBERS, LANES - VARS, LANES), f32)
-
-    def member(m, carry):
-        truths, pairs = carry
+    slope[...] = jnp.zeros((MEMBERS, LANES, LANES), f32)
+
+    def member(m, pairs):
         own = part[m]
-        off = own - truth
+        total = slope[m, :VARS, :]
+        for away in range(1, MEMBERS // 2 + 1):
+            k = (m + away) & (MEMBERS - 1)
+            between = own - part[k]
+            mean = jnp.sum(between * between, axis=0, keepdims=True) * (1.0 / VARS) + EPSILON
+            weight = lax.rsqrt(mean)
+            pull = between * weight
+            total = total + pull
+            if away < MEMBERS // 2:
+                slope[k, :VARS, :] = slope[k, :VARS, :] - pull
+                pairs = pairs + mean * weight
+            else:
+                pairs = pairs + (0.5 * mean) * weight
+        slope[m, :VARS, :] = total
+        return pairs
+
+    pairs = lax.fori_loop(0, MEMBERS, member, jnp.zeros((1, LANES), f32))
+    truths = jnp.zeros((1, LANES), f32)
+    for k in range(MEMBERS):
+        off = part[k] - truth
         mean = jnp.sum(off * off, axis=0, keepdims=True) * (1.0 / VARS) + EPSILON
         inverse = lax.rsqrt(mean)
         truths = truths + mean * inverse
-        total = jnp.zeros_like(own)
-        for k in range(MEMBERS):
-            between = own - part[k]
-            mean = jnp.sum(between * between, axis=0, keepdims=True) * (1.0 / VARS) + EPSILON
-            weight = lax.rsqrt(mean)
-            distinct = jnp.where(m == k, 0.0, 1.0)
-            pairs = pairs + (mean * weight) * distinct
-            total = total + between * weight
-        slope[m, :VARS, :] = off * (inverse * area * TRUTH_SCALE) - total * (area * PAIR_SCALE)
-        return truths, pairs
-
-    zero = jnp.zeros((1, LANES), f32)
-    truths, pairs = lax.fori_loop(0, MEMBERS, member, (zero, zero))
-    loss_ref[...] = area * (truths * (1.0 / MEMBERS) - pairs * (0.5 / PAIRS))
-    for k in range(MEMBERS):
+        own = off * (inverse * area * TRUTH_SCALE) - slope[k, :VARS, :] * (area * PAIR_SCALE)
+        slope[k, :VARS, :] = own
         grad[k // FOUR][:, (k % FOUR) * LANES : (k % FOUR + 1) * LANES] = slope[k].T.astype(bf16)
+    loss_ref[...] = area * (truths * (1.0 / MEMBERS) - pairs * (1.0 / PAIRS))
 
 
 def fine(place, truth, area, got):
@@ -358,7 +398,7 @@
     )(core, column, near_part, own, other)
 
 
-def backward_kernel(up_ref, preact_ref, wo_ref, w_ref, factor_ref, out_ref, wide, grads):
+def backward_kernel(up_ref, slope_ref, wo_ref, w_ref, factor_ref, out_ref, wide, grads):
     @pl.when(pl.program_id(0) == 0)
     def _():
         wide[:VARS, :] = wo_ref[...]
@@ -368,9 +408,7 @@
     step = 256
     for n in range(0, units, step):
         hidden = jnp.dot(up_ref[...], wide[:, n : n + step], preferred_element_type=f32)
-        pre = preact_ref[:, n : n + step]
-        sigma = 0.5 * jnp.tanh(0.5 * pre) + 0.5
-        slope = sigma * (1.0 + pre * (1.0 - sigma))
+        slope = slope_ref[:, n : n + step].astype(f32)
         grads[:, n : n + step] = (hidden * slope).astype(bf16)
     for n in range(0, w_ref.shape[0], step):
         total = lax.dot_general(
@@ -379,7 +417,7 @@
         out_ref[:, n : n + step] = (total * factor_ref[0:1, 0:1]).astype(bf16)
 
 
-def backward(up, preact, wo_t, w_in, factor, nodes):
+def backward(up, slope, wo_t, w_in, factor, nodes):
     width, units = w_in.shape
     return pl.pallas_call(
         backward_kernel,
@@ -394,11 +432,12 @@
         out_specs=pl.BlockSpec((nodes, width), lambda j: (j, 0)),
         out_shape=jax.ShapeDtypeStruct((FOUR * nodes, width), bf16),
         scratch_shapes=[pltpu.VMEM((LANES, units), bf16), pltpu.VMEM((nodes, units), bf16)],
+        compiler_params=fits(24),
         cost_estimate=pl.CostEstimate(
             flops=2 * FOUR * nodes * width * units, bytes_accessed=16 << 20, transcendentals=0
         ),
         name="backward",
-    )(up, preact, wo_t, w_in, factor)
+    )(up, slope, wo_t, w_in, factor)
 
 
 def turned(block, places):
@@ -416,13 +455,12 @@
     core = lax.axis_index("c").astype(jnp.int32)[None]
     swap = [(0, 1), (1, 0)]
 
-    preact, pred = forward(flat, w_in, b_in[None, :], wo_t, b_out[None, :], truth, area_row, nodes)
-    sent = cell_sums(core, cell, pred, True, bf16)
-    arrived = lax.ppermute(sent, "c", swap)
+    inputs = (flat, w_in, b_in[None, :], wo_t, b_out[None, :], truth, area_row, cell)
+    slope, pred = forward(*map(in_hbm, inputs), nodes)
+    arrived = lax.ppermute(pred, "c", swap)
     blocks = split(place, pred.reshape(FOUR, LANES, FOUR * LANES))
     parts = [blocks[0]] + [turned(blocks[k], k) for k in range(1, FOUR)]
-    kept = cell_sums(core, cell, pred, False, f32)
-    both = (kept + arrived.astype(f32)).astype(bf16).reshape(64, 8, FOUR * LANES)
+    both = theirs(core, ours(core, cell, pred), arrived).reshape(64, 8, FOUR * LANES)
     gathered = lax.all_to_all(both, WIDE, 0, 0, tiled=True)
     *grads, fine_loss = fine(place, truth, area_row, parts)
     grads = [grads[0]] + [turned(grads[k], -k) for k in range(1, FOUR)]
@@ -433,7 +471,7 @@
     other = lax.ppermute(own, "c", swap)
     near_part = near(core, column, base.reshape(nodes, FOUR * LANES), own)
     up, factor, scores = far(core, column, near_part, own, other)
-    latent_grad = backward(up, preact, wo_t, w_in, factor, nodes)
+    latent_grad = backward(up, in_hbm(slope), wo_t, w_in, factor, nodes)
     return (latent_grad.reshape(members, nodes, width), scores)
 
 

time: 92.3 us -> 88.3 us (0.957)
  local copies, waits for them, and re-layouts: 2.49 us -> 0.67 us
  other arithmetic: 1.01 us -> 0 us
  Pallas kernels: 26.5 us -> 25.5 us
    pallas_call x1, Pallas kernels: 10.4 us -> 8.45 us  [backward(): pl.pallas_call(backward_kernel, grid=(FOUR,), in_specs=[pl.BlockSpec((nod...]
    unnamed x14 -> x12, local copies, waits for them, and re-layouts: 2.49 us -> 0.67 us
    reshape x1 -> x0, other arithmetic: 1.01 us -> none  [shards(): (kept + arrived.astype(f32)).astype(bf16).reshape(64, 8, FOUR * LANES)]
  transfers between devices with their start and end apart: 9 -> 9, of which waited for: 6 -> 6; matrix products, arithmetic and copies ran while one was open for 0% -> 0% of each run, Pallas kernels for 5% -> 4%
where the time goes in v3:
time: 88.3 us; the launch traced here: 87.1 us
  Pallas kernels  25.5 us (29%)
  blocking collectives  20.8 us (24%)
  starting transfers between devices  20.2 us (23%)
  waiting for transfers between devices  19.2 us (22%)
    all_to_all x1, blocking collectives, shards(): own = lax.all_to_all(table, WIDE, 0, 0, tiled=True)  20.8 us
    ppermute x6, waiting for transfers between devices, turned(): lax.ppermute(block, 'm', [(j, (j + places) % FOUR) for j in range(FOUR)])  17.8 us
    all_to_all x1, starting transfers between devices, shards(): gathered = lax.all_to_all(both, WIDE, 0, 0, tiled=True)  11.5 us
    pallas_call x1, Pallas kernels, forward(): pl.pallas_call(forward_kernel, grid=(FOUR,), in_specs=[pl.BlockSpec((node...  10.9 us
    ppermute x6, starting transfers between devices, turned(): lax.ppermute(block, 'm', [(j, (j + places) % FOUR) for j in range(FOUR)])  8.55 us
    pallas_call x1, Pallas kernels, backward(): pl.pallas_call(backward_kernel, grid=(FOUR,), in_specs=[pl.BlockSpec((nod...  8.45 us
    pallas_call x1, Pallas kernels, fine(): pl.pallas_call(fine_kernel, in_specs=[smem()] + [vmem()] * 6, out_specs=[...  2.4 us
  transfers between devices with their start and end apart: 9, of which 6 were waited for; matrix products, arithmetic and copies ran while one was open for 0% of the time, Pallas kernels for 4%

profile of v3, /device:TPU:0, one launch (start us, length us, event | category | flops | bytes accessed | tf_op | source)
XLA Modules:
  0.0 87.1 jit_solution(1145250888391315853)
XLA Ops:
  0.6 10.9 %forward.1 = (bf16[2048,1024]{1,0:T(8,128)(2,1)}, bf16[512,512]{1,0:T(8,128)(2,1)S(1)}) custom-call(bf16[2048,1024]{1,0:T(8,128)(2,1)} %bitcast.29, bf16[1024,1024]{1,0:T(8,128)(2,1)} %w_ref.3, f32[1,1024]{1,0:T(1,128)} %bitcast.30, bf16[96,1024]{1,0:T(8,128)(2,1)} %bitcast.27, f32[1,96]{1,0:T(1,128)} %bitcast.31, f32[96,512]{1,0:T(8,128)} %bitcast.19, ...), custom_call_target="tpu_custom_call" | custom-call | flops 4294967296 | bytes 16777216 | tf_op jit(solution)/shard_map/forward/pallas_call | solution.py:80
  11.5 0.1 collective-permute-start.6
  11.6 0.0 copy-done.2
  11.6 0.4 ours.1.ours_ref
  12.1 1.4 %collective-permute-done.6.pred_ref = bf16[512,512]{1,0:T(8,128)(2,1)S(1)} collective-permute-done((bf16[512,512]{1,0:T(8,128)(2,1)S(1)}, bf16[512,512]{1,0:T(8,128)(2,1)S(1)}, u32[]{:S(2)}, u32[]{:S(2)}) %collective-permute-start.6) | collective-permute-done | bytes 524320 | tf_op jit(solution)/shard_map/ppermute | solution.py:460
  13.5 1.4 %theirs.1 = bf16[512,512]{1,0:T(8,128)(2,1)} custom-call(s32[1]{0:T(128)} %bitcast.core_ref, f32[512,512]{1,0:T(8,128)S(1)} %ours.1.ours_ref, bf16[512,512]{1,0:T(8,128)(2,1)S(1)} %collective-permute-done.6.pred_ref), custom_call_target="tpu_custom_call" | custom-call | flops 268435456 | bytes 2097152 | tf_op jit(solution)/shard_map/theirs/pallas_call | solution.py:149
  14.9 11.5 %all-to-all-start = ((bf16[64,8,512]{2,1,0:T(8,128)(2,1)}), bf16[64,8,512]{2,1,0:T(8,128)(2,1)S(1)}, u32[]{:S(2)}, u32[]{:S(2)}) async-start(bf16[64,8,512]{2,1,0:T(8,128)(2,1)} %bitcast.11), calls=%async_computation | async-start | bytes 1048576 | tf_op jit(solution)/shard_map/all_to_all | solution.py:464
  26.5 1.6 %collective-permute-start = (bf16[128,512]{1,0:T(8,128)(2,1)S(1)}, bf16[128,512]{1,0:T(8,128)(2,1)S(1)}, u32[]{:S(2)}, u32[]{:S(2)}) collective-permute-start(bf16[128,512]{1,0:T(8,128)(2,1)S(1)} %get-tuple-element.20), channel_id=1, source_target_pairs={{0,1},{1,2},{2,3},{3,0},{4,5},{5,6},{6,7},{7,4},{8,9},{9,10},{10,1... | collective-permute-start | bytes 393224 | tf_op jit(solution)/shard_map/ppermute | solution.py:444
  28.1 2.7 %collective-permute-start.1 = (bf16[128,512]{1,0:T(8,128)(2,1)S(1)}, bf16[128,512]{1,0:T(8,128)(2,1)S(1)}, u32[]{:S(2)}, u32[]{:S(2)}) collective-permute-start(bf16[128,512]{1,0:T(8,128)(2,1)S(1)} %get-tuple-element.21), channel_id=1, source_target_pairs={{0,2},{1,3},{2,0},{3,1},{4,6},{5,7},{6,4},{7,5},{8,10},{9,11},{10,... | collective-permute-start | bytes 393224 | tf_op jit(solution)/shard_map/ppermute | solution.py:444
  30.8 1.5 %collective-permute-start.2 = (bf16[128,512]{1,0:T(8,128)(2,1)S(1)}, bf16[128,512]{1,0:T(8,128)(2,1)S(1)}, u32[]{:S(2)}, u32[]{:S(2)}) collective-permute-start(bf16[128,512]{1,0:T(8,128)(2,1)S(1)} %get-tuple-element.22), channel_id=1, source_target_pairs={{0,3},{1,0},{2,1},{3,2},{4,7},{5,4},{6,5},{7,6},{8,11},{9,8},{10,9... | collective-permute-start | bytes 393224 | tf_op jit(solution)/shard_map/ppermute | solution.py:444
  32.2 5.7 %collective-permute-done.refs_1_ = bf16[128,512]{1,0:T(8,128)(2,1)S(1)} collective-permute-done((bf16[128,512]{1,0:T(8,128)(2,1)S(1)}, bf16[128,512]{1,0:T(8,128)(2,1)S(1)}, u32[]{:S(2)}, u32[]{:S(2)}) %collective-permute-start) | collective-permute-done | bytes 131104 | tf_op jit(solution)/shard_map/ppermute | solution.py:444
  38.0 3.9 %collective-permute-done.1.refs_2_ = bf16[128,512]{1,0:T(8,128)(2,1)S(1)} collective-permute-done((bf16[128,512]{1,0:T(8,128)(2,1)S(1)}, bf16[128,512]{1,0:T(8,128)(2,1)S(1)}, u32[]{:S(2)}, u32[]{:S(2)}) %collective-permute-start.1) | collective-permute-done | bytes 131104 | tf_op jit(solution)/shard_map/ppermute | solution.py:444
  41.9 0.0 collective-permute-done.2.refs_3_
  41.9 0.0 copy-start.3
  41.9 0.0 copy-start.4
  41.9 2.4 %fine.1 = (bf16[128,512]{1,0:T(8,128)(2,1)S(1)}, bf16[128,512]{1,0:T(8,128)(2,1)S(1)}, bf16[128,512]{1,0:T(8,128)(2,1)S(1)}, bf16[128,512]{1,0:T(8,128)(2,1)S(1)}, f32[1,128]{1,0:T(1,128)S(1)}) custom-call(s32[1]{0:T(128)} %bitcast.1.place_ref, f32[96,512]{1,0:T(8,128)S(1)} %bitcast.20, f32[1,512]{1,0:T(1,128)S(1)} %bitcast.22, ...), custom_call_target="tpu_custom_call" | custom-call | flops 50331648 | bytes 2097152 | tf_op jit(solution)/shard_map/fine/pallas_call | solution.py:223
  44.3 0.6 copy-done.5
  45.0 0.0 all-to-all-done.got_ref
  45.0 0.4 coarse.1
  45.4 20.8 %all_to_all.10 = bf16[64,8,512]{2,1,0:T(8,128)(2,1)S(1)} all-to-all(bf16[64,8,512]{2,1,0:T(8,128)(2,1)S(1)} %coarse.1), channel_id=1, replica_groups=mesh['x'=4,'y'=4,'c'=2,'m'=4] {'x','y','m'}, dimensions={0} | all-to-all | bytes 1048576 | tf_op jit(solution)/shard_map/all_to_all | solution.py:468
  66.2 0.0 collective-permute-start.7
  66.2 1.0 %collective-permute-start.3 = (bf16[128,512]{1,0:T(8,128)(2,1)}, bf16[128,512]{1,0:T(8,128)(2,1)S(1)}, u32[]{:S(2)}, u32[]{:S(2)}) collective-permute-start(bf16[128,512]{1,0:T(8,128)(2,1)} %copy-done.5), channel_id=1, source_target_pairs={{0,3},{1,0},{2,1},{3,2},{4,7},{5,4},{6,5},{7,6},{8,11},{9,8},{10,9... | collective-permute-start | bytes 393224 | tf_op jit(solution)/shard_map/ppermute | solution.py:444
  67.2 1.7 %collective-permute-start.4 = (bf16[128,512]{1,0:T(8,128)(2,1)S(1)}, bf16[128,512]{1,0:T(8,128)(2,1)S(1)}, u32[]{:S(2)}, u32[]{:S(2)}) collective-permute-start(bf16[128,512]{1,0:T(8,128)(2,1)S(1)} %get-tuple-element.25), channel_id=1, source_target_pairs={{0,2},{1,3},{2,0},{3,1},{4,6},{5,7},{6,4},{7,5},{8,10},{9,11},{10,... | collective-permute-start | bytes 393224 | tf_op jit(solution)/shard_map/ppermute | solution.py:444
  68.9 0.1 collective-permute-start.5
  69.0 3.8 %collective-permute-done.3.refs_1_ = bf16[128,512]{1,0:T(8,128)(2,1)S(1)} collective-permute-done((bf16[128,512]{1,0:T(8,128)(2,1)}, bf16[128,512]{1,0:T(8,128)(2,1)S(1)}, u32[]{:S(2)}, u32[]{:S(2)}) %collective-permute-start.3) | collective-permute-done | bytes 131104 | tf_op jit(solution)/shard_map/ppermute | solution.py:444
  72.8 2.3 %collective-permute-done.4.refs_2_ = bf16[128,512]{1,0:T(8,128)(2,1)S(1)} collective-permute-done((bf16[128,512]{1,0:T(8,128)(2,1)S(1)}, bf16[128,512]{1,0:T(8,128)(2,1)S(1)}, u32[]{:S(2)}, u32[]{:S(2)}) %collective-permute-start.4) | collective-permute-done | bytes 131104 | tf_op jit(solution)/shard_map/ppermute | solution.py:444
  75.0 2.1 %collective-permute-done.5.refs_3_ = bf16[128,512]{1,0:T(8,128)(2,1)S(1)} collective-permute-done((bf16[128,512]{1,0:T(8,128)(2,1)S(1)}, bf16[128,512]{1,0:T(8,128)(2,1)S(1)}, u32[]{:S(2)}, u32[]{:S(2)}) %collective-permute-start.5) | collective-permute-done | bytes 131104 | tf_op jit(solution)/shard_map/ppermute | solution.py:444
  77.1 0.1 base.1
  77.3 0.4 near.1.near_ref
  77.7 0.0 collective-permute-done.7.other_ref
  77.7 0.9 %far.1 = (bf16[512,512]{1,0:T(8,128)(2,1)S(1)}, f32[1,128]{1,0:T(1,128)S(1)}, f32[2]{0:T(128)}) custom-call(s32[1]{0:T(128)} %bitcast.core_ref, f32[512,128]{1,0:T(8,128)S(1)} %get-tuple-element.27.column_ref, f32[512,512]{1,0:T(8,128)S(1)} %near.1.near_ref, bf16[512,512]{1,0:T(8,128)(2,1)S(1)} %bitcast.16, bf16[512,512]{1,0:T(8,128)(2,1)S(1)} %collective-permute-done.7.other_ref), custom_call_target="tpu_custom_call" | custom-call | tf_op jit(solution)/shard_map/far/pallas_call | solution.py:387
  78.6 8.5 %backward.1 = bf16[2048,1024]{1,0:T(8,128)(2,1)} custom-call(bf16[512,512]{1,0:T(8,128)(2,1)S(1)} %get-tuple-element.30.up_ref, bf16[2048,1024]{1,0:T(8,128)(2,1)} %get-tuple-element.31.slope_ref, bf16[96,1024]{1,0:T(8,128)(2,1)S(1)} %bitcast.28, bf16[1024,1024]{1,0:T(8,128)(2,1)S(1)} %copy-done.3, f32[1,128]{1,0:T(1,128)S(1)} %get-tuple-element.32.factor_ref), custom_call_target="tpu_custom_call" | custom-call | flops 4294967296 | bytes 16777216 | tf_op jit(solution)/shard_map/backward/pallas_call | solution.py:422
  (9 shorter events, 0.1 us)
Async XLA Ops:
  0.6 11.0 %copy-start.2 = (s32[512]{0:T(512)S(1)}, s32[512]{0:T(512)}, u32[]{:S(2)}) copy-start(s32[512]{0:T(512)} %param.15) | copy-start | bytes 6148
  11.5 30.4 %copy-start = (f32[512,96]{0,1:T(8,128)S(1)}, f32[512,96]{0,1:T(8,128)}, u32[]{:S(2)}) copy-start(f32[512,96]{0,1:T(8,128)} %param.13) | copy-start | bytes 589828
  11.5 30.4 %copy-start.1 = (f32[512]{0:T(512)S(1)}, f32[512]{0:T(512)}, u32[]{:S(2)}) copy-start(f32[512]{0:T(512)} %param.14) | copy-start | bytes 6148
  11.5 2.0 %collective-permute-start.6 = (bf16[512,512]{1,0:T(8,128)(2,1)S(1)}, bf16[512,512]{1,0:T(8,128)(2,1)S(1)}, u32[]{:S(2)}, u32[]{:S(2)}) collective-permute-start(bf16[512,512]{1,0:T(8,128)(2,1)S(1)} %get-tuple-element.18.pred_ref), channel_id=1, source_target_pairs={{0,4},{4,0},{1,5},{5,1},{2,6},{6,2},{3,7},{7,3},{8,12},{12,8},{9,1... | collective-permute-start | bytes 1572872 | tf_op jit(solution)/shard_map/ppermute | solution.py:460
  14.9 30.1 %all-to-all-start = ((bf16[64,8,512]{2,1,0:T(8,128)(2,1)}), bf16[64,8,512]{2,1,0:T(8,128)(2,1)S(1)}, u32[]{:S(2)}, u32[]{:S(2)}) async-start(bf16[64,8,512]{2,1,0:T(8,128)(2,1)} %bitcast.11), calls=%async_computation | async-start | bytes 1048576 | tf_op jit(solution)/shard_map/all_to_all | solution.py:464
  26.5 11.5 %collective-permute-start = (bf16[128,512]{1,0:T(8,128)(2,1)S(1)}, bf16[128,512]{1,0:T(8,128)(2,1)S(1)}, u32[]{:S(2)}, u32[]{:S(2)}) collective-permute-start(bf16[128,512]{1,0:T(8,128)(2,1)S(1)} %get-tuple-element.20), channel_id=1, source_target_pairs={{0,1},{1,2},{2,3},{3,0},{4,5},{5,6},{6,7},{7,4},{8,9},{9,10},{10,1... | collective-permute-start | bytes 393224 | tf_op jit(solution)/shard_map/ppermute | solution.py:444
  28.1 13.8 %collective-permute-start.1 = (bf16[128,512]{1,0:T(8,128)(2,1)S(1)}, bf16[128,512]{1,0:T(8,128)(2,1)S(1)}, u32[]{:S(2)}, u32[]{:S(2)}) collective-permute-start(bf16[128,512]{1,0:T(8,128)(2,1)S(1)} %get-tuple-element.21), channel_id=1, source_target_pairs={{0,2},{1,3},{2,0},{3,1},{4,6},{5,7},{6,4},{7,5},{8,10},{9,11},{10,... | collective-permute-start | bytes 393224 | tf_op jit(solution)/shard_map/ppermute | solution.py:444
  30.8 11.1 %collective-permute-start.2 = (bf16[128,512]{1,0:T(8,128)(2,1)S(1)}, bf16[128,512]{1,0:T(8,128)(2,1)S(1)}, u32[]{:S(2)}, u32[]{:S(2)}) collective-permute-start(bf16[128,512]{1,0:T(8,128)(2,1)S(1)} %get-tuple-element.22), channel_id=1, source_target_pairs={{0,3},{1,0},{2,1},{3,2},{4,7},{5,4},{6,5},{7,6},{8,11},{9,8},{10,9... | collective-permute-start | bytes 393224 | tf_op jit(solution)/shard_map/ppermute | solution.py:444
  41.9 36.7 %copy-start.3 = (bf16[1024,1024]{1,0:T(8,128)(2,1)S(1)}, bf16[1024,1024]{1,0:T(8,128)(2,1)}, u32[]{:S(2)}) copy-start(bf16[1024,1024]{1,0:T(8,128)(2,1)} %w_ref.3) | copy-start | bytes 6291460
  41.9 36.7 %copy-start.4 = (bf16[1024,96]{0,1:T(8,128)(2,1)S(1)}, bf16[1024,96]{0,1:T(8,128)(2,1)}, u32[]{:S(2)}) copy-start(bf16[1024,96]{0,1:T(8,128)(2,1)} %param.11) | copy-start | bytes 589828
  44.3 0.7 copy-start.5
  66.2 11.5 %collective-permute-start.7 = (bf16[512,512]{1,0:T(8,128)(2,1)S(1)}, bf16[512,512]{1,0:T(8,128)(2,1)S(1)}, u32[]{:S(2)}, u32[]{:S(2)}) collective-permute-start(bf16[512,512]{1,0:T(8,128)(2,1)S(1)} %bitcast.14), channel_id=1, source_target_pairs={{0,4},{4,0},{1,5},{5,1},{2,6},{6,2},{3,7},{7,3},{8,12},{12,8},{9,1... | collective-permute-start | bytes 1572872 | tf_op jit(solution)/shard_map/ppermute | solution.py:471
  66.2 6.6 %collective-permute-start.3 = (bf16[128,512]{1,0:T(8,128)(2,1)}, bf16[128,512]{1,0:T(8,128)(2,1)S(1)}, u32[]{:S(2)}, u32[]{:S(2)}) collective-permute-start(bf16[128,512]{1,0:T(8,128)(2,1)} %copy-done.5), channel_id=1, source_target_pairs={{0,3},{1,0},{2,1},{3,2},{4,7},{5,4},{6,5},{7,6},{8,11},{9,8},{10,9... | collective-permute-start | bytes 393224 | tf_op jit(solution)/shard_map/ppermute | solution.py:444
  67.2 7.9 %collective-permute-start.4 = (bf16[128,512]{1,0:T(8,128)(2,1)S(1)}, bf16[128,512]{1,0:T(8,128)(2,1)S(1)}, u32[]{:S(2)}, u32[]{:S(2)}) collective-permute-start(bf16[128,512]{1,0:T(8,128)(2,1)S(1)} %get-tuple-element.25), channel_id=1, source_target_pairs={{0,2},{1,3},{2,0},{3,1},{4,6},{5,7},{6,4},{7,5},{8,10},{9,11},{10,... | collective-permute-start | bytes 393224 | tf_op jit(solution)/shard_map/ppermute | solution.py:444
  68.9 8.2 %collective-permute-start.5 = (bf16[128,512]{1,0:T(8,128)(2,1)S(1)}, bf16[128,512]{1,0:T(8,128)(2,1)S(1)}, u32[]{:S(2)}, u32[]{:S(2)}) collective-permute-start(bf16[128,512]{1,0:T(8,128)(2,1)S(1)} %get-tuple-element.26), channel_id=1, source_target_pairs={{0,1},{1,2},{2,3},{3,0},{4,5},{5,6},{6,7},{7,4},{8,9},{9,10},{10,1... | collective-permute-start | bytes 393224 | tf_op jit(solution)/shard_map/ppermute | solution.py:444

commit v4 on v3

--- a/solution.py
+++ b/solution.py
@@ -66,13 +66,22 @@
     features = jnp.where(j < 2, ones, jnp.where(j == 2, spread, ids))
     extra[VARS : VARS + 24, :] = truth_ref[pl.ds(pl.multiple_of(24 * j, 8), 24), :]
     extra[VARS + 24 :, :] = features
-    pre = jnp.dot(x_ref[...], w_ref[...], preferred_element_type=f32) + b_ref[...]
-    sigma = 0.5 * jnp.tanh(0.5 * pre) + 0.5
-    silu = pre * sigma
-    slope_ref[...] = (sigma + silu * (1.0 - sigma)).astype(bf16)
-    act = silu.astype(bf16)
-    total = lax.dot_general(act, wide[...], (((1,), (1,)), ((), ())), preferred_element_type=f32)
-    pred_ref[...] = (total + bias[...] + extra[...].T).astype(bf16)
+    turned_extra = extra[...].T
+    halves = 2
+    rows = nodes // halves
+    products = [
+        jnp.dot(x_ref[k * rows : (k + 1) * rows, :], w_ref[...], preferred_element_type=f32)
+        for k in range(halves)
+    ]
+    for k in range(halves):
+        here = slice(k * rows, (k + 1) * rows)
+        pre = products[k] + b_ref[...]
+        sigma = 0.5 * jnp.tanh(0.5 * pre) + 0.5
+        silu = pre * sigma
+        slope_ref[here, :] = (sigma + silu * (1.0 - sigma)).astype(bf16)
+        act = silu.astype(bf16)
+        total = lax.dot_general(act, wide[...], (((1,), (1,)), ((), ())), preferred_element_type=f32)
+        pred_ref[here, :] = (total + bias[...] + turned_extra[here, :]).astype(bf16)
 
 
 def forward(flat, w_in, b_in, wo_t, b_out, truth, area, cell, nodes):
@@ -117,46 +126,29 @@
     return jnp.dot(picker, pred, preferred_element_type=f32)
 
 
-def ours_kernel(core_ref, cell_ref, pred_ref, out_ref):
-    out_ref[...] = gathered_rows(core_ref[0], cell_ref[...], pred_ref[...])
-
-
-def ours(core, cell, pred):
-    return pl.pallas_call(
-        ours_kernel,
-        in_specs=[smem(), vmem(), vmem()],
+def cells_kernel(core_ref, cell_ref, pred_ref, other_ref, out_ref):
+    lane = lax.broadcasted_iota(jnp.int32, (8, LANES), 1)
+    digits = jnp.where(lane == VARS + 24, 32.0, jnp.where(lane == VARS + 25, 1.0, 0.0)).astype(bf16)
+    last = other_ref[:, (FOUR - 1) * LANES :]
+    ids = lax.dot_general(digits, last, (((1,), (1,)), ((), ())), preferred_element_type=f32)
+    ids = ids[0:1, :].astype(jnp.int32)
+    core = core_ref[0]
+    total = gathered_rows(core, cell_ref[...], pred_ref[...])
+    out_ref[...] = (total + gathered_rows(core, ids, other_ref[...])).astype(bf16)
+
+
+def cell_sums(core, cell, pred, other):
+    return pl.pallas_call(
+        cells_kernel,
+        in_specs=[smem(), vmem(), vmem(), vmem()],
         out_specs=vmem(),
-        out_shape=jax.ShapeDtypeStruct((HALF, pred.shape[1]), f32),
+        out_shape=jax.ShapeDtypeStruct((HALF, pred.shape[1]), bf16),
         compiler_params=fits(8),
         cost_estimate=pl.CostEstimate(
-            flops=2 * HALF * pred.size, bytes_accessed=2 << 20, transcendentals=0
+            flops=4 * HALF * pred.size, bytes_accessed=2 << 20, transcendentals=0
         ),
-        name="ours",
-    )(core, cell, pred)
-
-
-def theirs_kernel(core_ref, ours_ref, pred_ref, out_ref):
-    lane = lax.broadcasted_iota(jnp.int32, (8, LANES), 1)
-    digits = jnp.where(lane == VARS + 24, 32.0, jnp.where(lane == VARS + 25, 1.0, 0.0)).astype(bf16)
-    last = pred_ref[:, (FOUR - 1) * LANES :]
-    ids = lax.dot_general(digits, last, (((1,), (1,)), ((), ())), preferred_element_type=f32)
-    ids = ids[0:1, :].astype(jnp.int32)
-    total = ours_ref[...] + gathered_rows(core_ref[0], ids, pred_ref[...])
-    out_ref[...] = total.astype(bf16)
-
-
-def theirs(core, partial, pred):
-    return pl.pallas_call(
-        theirs_kernel,
-        in_specs=[smem(), vmem(), vmem()],
-        out_specs=vmem(),
-        out_shape=jax.ShapeDtypeStruct(partial.shape, bf16),
-        compiler_params=fits(8),
-        cost_estimate=pl.CostEstimate(
-            flops=2 * HALF * pred.size, bytes_accessed=2 << 20, transcendentals=0
-        ),
-        name="theirs",
-    )(core, partial, pred)
+        name="cells",
+    )(core, cell, pred, other)
 
 
 def split_kernel(place_ref, pred_ref, *out_refs):
@@ -315,62 +307,83 @@
     )(got, loss, area)
 
 
-def picked(half, column, table):
-    first = (half * HALF).astype(f32)
-    ids = lax.broadcasted_iota(jnp.int32, (column.shape[0], HALF), 1).astype(f32) + first
+def base_kernel(place_ref, core_ref, cell_ref, *refs):
+    got, base_ref, near_ref, far_ref = refs[:4], refs[4], refs[5], refs[6]
+    nodes = cell_ref.shape[1]
+    column = jnp.broadcast_to(cell_ref[...].astype(f32), (LANES, nodes)).T
     wide = jnp.concatenate([column] * (HALF // LANES), axis=1)
-    picker = jnp.where(ids == wide, 1.0, 0.0).astype(bf16)
-    return jnp.dot(picker, table, preferred_element_type=f32)
-
-
-def base_kernel(place_ref, cell_ref, *refs):
-    got, base_ref, column_ref = refs[:4], refs[4], refs[5]
-    nodes = cell_ref.shape[1]
-    column_ref[...] = jnp.broadcast_to(cell_ref[...].astype(f32), (LANES, nodes)).T
+    for picker_ref, half in ((near_ref, core_ref[0]), (far_ref, 1 - core_ref[0])):
+        ids = (lax.broadcasted_iota(jnp.int32, (nodes, HALF), 1) + half * HALF).astype(f32)
+        picker_ref[...] = jnp.where(ids == wide, 1.0, 0.0).astype(bf16)
     for k in range(FOUR):
         base_ref[(place_ref[0] + k) & 3] = got[k][...].astype(f32)
 
 
-def based(place, cell, got):
+def based(place, core, cell, got):
     return pl.pallas_call(
         base_kernel,
-        in_specs=[smem()] + [vmem()] * 5,
-        out_specs=[vmem(), vmem()],
+        in_specs=[smem(), smem()] + [vmem()] * 5,
+        out_specs=[vmem()] * 3,
         out_shape=[
             jax.ShapeDtypeStruct((FOUR, *got[0].shape), f32),
-            jax.ShapeDtypeStruct((cell.shape[1], LANES), f32),
-        ],
-        compiler_params=fits(6),
+            jax.ShapeDtypeStruct((cell.shape[1], HALF), bf16),
+            jax.ShapeDtypeStruct((cell.shape[1], HALF), bf16),
+        ],
+        compiler_params=fits(8),
         cost_estimate=pl.CostEstimate(flops=1 << 20, bytes_accessed=2 << 20, transcendentals=0),
         name="base",
-    )(place, cell, *got)
-
-
-def near_kernel(core_ref, column_ref, base_ref, table_ref, out_ref):
-    out_ref[...] = base_ref[...] + picked(core_ref[0], column_ref[...], table_ref[...])
-
-
-def near(core, column, base, table):
+    )(place, core, cell, *got)
+
+
+def spare_sums(table_ref):
+    return jnp.sum(table_ref[:, :LANES].astype(f32), axis=0, keepdims=True)
+
+
+def near_kernel(picker_ref, base_ref, table_ref, out_ref, sums_ref):
+    picked = jnp.dot(picker_ref[...], table_ref[...], preferred_element_type=f32)
+    out_ref[...] = base_ref[...] + picked
+    sums_ref[...] = spare_sums(table_ref)
+
+
+def near(picker, base, table):
     return pl.pallas_call(
         near_kernel,
-        in_specs=[smem(), vmem(), vmem(), vmem()],
-        out_specs=vmem(),
-        out_shape=jax.ShapeDtypeStruct(base.shape, f32),
+        in_specs=[vmem()] * 3,
+        out_specs=[vmem()] * 2,
+        out_shape=[
+            jax.ShapeDtypeStruct(base.shape, f32),
+            jax.ShapeDtypeStruct((1, LANES), f32),
+        ],
         compiler_params=fits(8),
         cost_estimate=pl.CostEstimate(
             flops=2 * HALF * table.size, bytes_accessed=2 << 20, transcendentals=0
         ),
         name="near",
-    )(core, column, base, table)
-
-
-def far_kernel(
-    core_ref, column_ref, near_ref, own_ref, other_ref, up_ref, factor_ref, score_ref
-):
-    total = near_ref[...] + picked(1 - core_ref[0], column_ref[...], other_ref[...])
-    up_ref[...] = total.astype(bf16)
-    sums = own_ref[:, :LANES].astype(f32) + other_ref[:, :LANES].astype(f32)
-    sums = jnp.sum(sums, axis=0, keepdims=True)
+    )(picker, base, table)
+
+
+def far_kernel(picker_ref, near_ref, near_sums_ref, table_ref, up_ref, sums_ref):
+    picked = jnp.dot(picker_ref[...], table_ref[...], preferred_element_type=f32)
+    up_ref[...] = (near_ref[...] + picked).astype(bf16)
+    sums_ref[...] = near_sums_ref[...] + spare_sums(table_ref)
+
+
+def far(picker, near_part, near_sums, table):
+    return pl.pallas_call(
+        far_kernel,
+        in_specs=[vmem()] * 4,
+        out_specs=[vmem(), vmem()],
+        compiler_params=fits(8),
+        out_shape=[
+            jax.ShapeDtypeStruct(near_part.shape, bf16),
+            jax.ShapeDtypeStruct((1, LANES), f32),
+        ],
+        name="far",
+    )(picker, near_part, near_sums, table)
+
+
+def backward_kernel(up_ref, slope_ref, wo_ref, w_ref, sums_ref, out_ref, score_ref, wide, grads):
+    sums = sums_ref[...]
     lane = lax.broadcasted_iota(jnp.int32, (1, LANES), 1)
 
     def of(index):
@@ -378,29 +391,12 @@
         return jnp.sum(jnp.where(here, sums, 0.0), axis=1, keepdims=True)
 
     area = of(2) * (1.0 / FOUR)
-    factor_ref[...] = jnp.broadcast_to(LOSS_SCALE * NODE_TOTAL / area, (1, LANES))
-    score_ref[0] = (of(0) / area)[0, 0]
-    score_ref[1] = (of(1) / area)[0, 0]
-
-
-def far(core, column, near_part, own, other):
-    return pl.pallas_call(
-        far_kernel,
-        in_specs=[smem()] + [vmem()] * 4,
-        out_specs=[vmem(), vmem(), smem()],
-        compiler_params=fits(10),
-        out_shape=[
-            jax.ShapeDtypeStruct(near_part.shape, bf16),
-            jax.ShapeDtypeStruct((1, LANES), f32),
-            jax.ShapeDtypeStruct((2,), f32),
-        ],
-        name="far",
-    )(core, column, near_part, own, other)
-
-
-def backward_kernel(up_ref, slope_ref, wo_ref, w_ref, factor_ref, out_ref, wide, grads):
+    factor = LOSS_SCALE * NODE_TOTAL / area
+
     @pl.when(pl.program_id(0) == 0)
     def _():
+        score_ref[0] = (of(0) / area)[0, 0]
+        score_ref[1] = (of(1) / area)[0, 0]
         wide[:VARS, :] = wo_ref[...]
         wide[VARS:, :] = jnp.zeros((LANES - VARS, wide.shape[1]), bf16)
 
@@ -414,10 +410,10 @@
         total = lax.dot_general(
             grads[...], w_ref[n : n + step, :], (((1,), (1,)), ((), ())), preferred_element_type=f32
         )
-        out_ref[:, n : n + step] = (total * factor_ref[0:1, 0:1]).astype(bf16)
-
-
-def backward(up, slope, wo_t, w_in, factor, nodes):
+        out_ref[:, n : n + step] = (total * factor).astype(bf16)
+
+
+def backward(up, slope, wo_t, w_in, sums, nodes):
     width, units = w_in.shape
     return pl.pallas_call(
         backward_kernel,
@@ -429,15 +425,18 @@
             pl.BlockSpec((width, units), lambda j: (0, 0)),
             pl.BlockSpec((1, LANES), lambda j: (0, 0)),
         ],
-        out_specs=pl.BlockSpec((nodes, width), lambda j: (j, 0)),
-        out_shape=jax.ShapeDtypeStruct((FOUR * nodes, width), bf16),
+        out_specs=[pl.BlockSpec((nodes, width), lambda j: (j, 0)), smem()],
+        out_shape=[
+            jax.ShapeDtypeStruct((FOUR * nodes, width), bf16),
+            jax.ShapeDtypeStruct((2,), f32),
+        ],
         scratch_shapes=[pltpu.VMEM((LANES, units), bf16), pltpu.VMEM((nodes, units), bf16)],
         compiler_params=fits(24),
         cost_estimate=pl.CostEstimate(
             flops=2 * FOUR * nodes * width * units, bytes_accessed=16 << 20, transcendentals=0
         ),
         name="backward",
-    )(up, slope, wo_t, w_in, factor)
+    )(up, slope, wo_t, w_in, sums)
 
 
 def turned(block, places):
@@ -460,18 +459,18 @@
     arrived = lax.ppermute(pred, "c", swap)
     blocks = split(place, pred.reshape(FOUR, LANES, FOUR * LANES))
     parts = [blocks[0]] + [turned(blocks[k], k) for k in range(1, FOUR)]
-    both = theirs(core, ours(core, cell, pred), arrived).reshape(64, 8, FOUR * LANES)
+    both = cell_sums(core, cell, pred, arrived).reshape(64, 8, FOUR * LANES)
     gathered = lax.all_to_all(both, WIDE, 0, 0, tiled=True)
     *grads, fine_loss = fine(place, truth, area_row, parts)
     grads = [grads[0]] + [turned(grads[k], -k) for k in range(1, FOUR)]
     table = coarse(gathered, fine_loss, area_row)
     own = lax.all_to_all(table, WIDE, 0, 0, tiled=True)
     own = own.reshape(HALF, FOUR * LANES)
-    base, column = based(place, cell, grads)
+    base, near_picker, far_picker = based(place, core, cell, grads)
     other = lax.ppermute(own, "c", swap)
-    near_part = near(core, column, base.reshape(nodes, FOUR * LANES), own)
-    up, factor, scores = far(core, column, near_part, own, other)
-    latent_grad = backward(up, in_hbm(slope), wo_t, w_in, factor, nodes)
+    near_part, near_sums = near(near_picker, base.reshape(nodes, FOUR * LANES), own)
+    up, sums = far(far_picker, near_part, near_sums, other)
+    latent_grad, scores = backward(up, in_hbm(slope), wo_t, w_in, sums, nodes)
     return (latent_grad.reshape(members, nodes, width), scores)
 
 

time: 88.3 us -> 87.9 us (level)
    pallas_call x5 -> x4, Pallas kernels: 3.27 us -> 2.8 us  [the longest x1 1.62 us: cell_sums(): pl.pallas_call(cells_kernel, in_specs=[smem(), vmem(), vmem(), vmem()], o...]
where the time goes in v4:
time: 87.9 us; the launch traced here: 86.8 us
  Pallas kernels  24.7 us (28%)
  blocking collectives  20.8 us (24%)
  starting transfers between devices  20.1 us (23%)
  waiting for transfers between devices  19.7 us (22%)
    all_to_all x1, blocking collectives, shards(): own = lax.all_to_all(table, WIDE, 0, 0, tiled=True)  20.8 us
    ppermute x6, waiting for transfers between devices, turned(): lax.ppermute(block, 'm', [(j, (j + places) % FOUR) for j in range(FOUR)])  17.8 us
    all_to_all x1, starting transfers between devices, shards(): gathered = lax.all_to_all(both, WIDE, 0, 0, tiled=True)  11.5 us
    pallas_call x1, Pallas kernels, forward(): pl.pallas_call(forward_kernel, grid=(FOUR,), in_specs=[pl.BlockSpec((node...  10.3 us
    pallas_call x1, Pallas kernels, backward(): pl.pallas_call(backward_kernel, grid=(FOUR,), in_specs=[pl.BlockSpec((nod...  8.82 us
    ppermute x6, starting transfers between devices, turned(): lax.ppermute(block, 'm', [(j, (j + places) % FOUR) for j in range(FOUR)])  8.55 us
    pallas_call x1, Pallas kernels, fine(): pl.pallas_call(fine_kernel, in_specs=[smem()] + [vmem()] * 6, out_specs=[...  2.4 us
    ppermute x1, waiting for transfers between devices, shards(): arrived = lax.ppermute(pred, 'c', swap)  1.91 us
  transfers between devices with their start and end apart: 9, of which 6 were waited for; matrix products, arithmetic and copies ran while one was open for 0% of the time, Pallas kernels for 4%

profile of v4, /device:TPU:0, one launch (start us, length us, event | category | flops | bytes accessed | tf_op | source)
XLA Modules:
  0.0 86.8 jit_solution(7113286138932324293)
XLA Ops:
  0.6 0.0 copy-start.2
  0.6 0.0 copy-start
  0.7 10.3 %forward.1 = (bf16[2048,1024]{1,0:T(8,128)(2,1)}, bf16[512,512]{1,0:T(8,128)(2,1)S(1)}) custom-call(bf16[2048,1024]{1,0:T(8,128)(2,1)} %bitcast.28, bf16[1024,1024]{1,0:T(8,128)(2,1)} %w_ref.3, f32[1,1024]{1,0:T(1,128)} %bitcast.29, bf16[96,1024]{1,0:T(8,128)(2,1)} %bitcast.26, f32[1,96]{1,0:T(1,128)} %bitcast.30, f32[96,512]{1,0:T(8,128)} %bitcast.18, ...), custom_call_target="tpu_custom_call" | custom-call | flops 4294967296 | bytes 16777216 | tf_op jit(solution)/shard_map/forward/pallas_call | solution.py:89
  10.9 0.0 collective-permute-start.6
  10.9 1.9 %collective-permute-done.6.other_ref = bf16[512,512]{1,0:T(8,128)(2,1)S(1)} collective-permute-done((bf16[512,512]{1,0:T(8,128)(2,1)S(1)}, bf16[512,512]{1,0:T(8,128)(2,1)S(1)}, u32[]{:S(2)}, u32[]{:S(2)}) %collective-permute-start.6) | collective-permute-done | bytes 524320 | tf_op jit(solution)/shard_map/ppermute | solution.py:459
  12.8 1.6 %cells.1 = bf16[512,512]{1,0:T(8,128)(2,1)} custom-call(s32[1]{0:T(128)} %bitcast.1.core_ref, s32[1,512]{1,0:T(1,128)S(1)} %bitcast.24, bf16[512,512]{1,0:T(8,128)(2,1)S(1)} %get-tuple-element.22.pred_ref, bf16[512,512]{1,0:T(8,128)(2,1)S(1)} %collective-permute-done.6.other_ref), custom_call_target="tpu_custom_call" | custom-call | flops 536870912 | bytes 2097152 | tf_op jit(solution)/shard_map/cells/pallas_call | solution.py:141
  14.5 11.5 %all-to-all-start = ((bf16[64,8,512]{2,1,0:T(8,128)(2,1)}), bf16[64,8,512]{2,1,0:T(8,128)(2,1)S(1)}, u32[]{:S(2)}, u32[]{:S(2)}) async-start(bf16[64,8,512]{2,1,0:T(8,128)(2,1)} %bitcast.11), calls=%async_computation | async-start | bytes 1048576 | tf_op jit(solution)/shard_map/all_to_all | solution.py:463
  26.0 0.0 copy-start.3
  26.0 0.0 copy-start.4
  26.1 1.6 %collective-permute-start = (bf16[128,512]{1,0:T(8,128)(2,1)S(1)}, bf16[128,512]{1,0:T(8,128)(2,1)S(1)}, u32[]{:S(2)}, u32[]{:S(2)}) collective-permute-start(bf16[128,512]{1,0:T(8,128)(2,1)S(1)} %get-tuple-element.24), channel_id=1, source_target_pairs={{0,1},{1,2},{2,3},{3,0},{4,5},{5,6},{6,7},{7,4},{8,9},{9,10},{10,1... | collective-permute-start | bytes 393224 | tf_op jit(solution)/shard_map/ppermute | solution.py:443
  27.7 2.7 %collective-permute-start.1 = (bf16[128,512]{1,0:T(8,128)(2,1)S(1)}, bf16[128,512]{1,0:T(8,128)(2,1)S(1)}, u32[]{:S(2)}, u32[]{:S(2)}) collective-permute-start(bf16[128,512]{1,0:T(8,128)(2,1)S(1)} %get-tuple-element.25), channel_id=1, source_target_pairs={{0,2},{1,3},{2,0},{3,1},{4,6},{5,7},{6,4},{7,5},{8,10},{9,11},{10,... | collective-permute-start | bytes 393224 | tf_op jit(solution)/shard_map/ppermute | solution.py:443
  30.4 1.5 %collective-permute-start.2 = (bf16[128,512]{1,0:T(8,128)(2,1)S(1)}, bf16[128,512]{1,0:T(8,128)(2,1)S(1)}, u32[]{:S(2)}, u32[]{:S(2)}) collective-permute-start(bf16[128,512]{1,0:T(8,128)(2,1)S(1)} %get-tuple-element.26), channel_id=1, source_target_pairs={{0,3},{1,0},{2,1},{3,2},{4,7},{5,4},{6,5},{7,6},{8,11},{9,8},{10,9... | collective-permute-start | bytes 393224 | tf_op jit(solution)/shard_map/ppermute | solution.py:443
  31.9 5.8 %collective-permute-done.refs_1_ = bf16[128,512]{1,0:T(8,128)(2,1)S(1)} collective-permute-done((bf16[128,512]{1,0:T(8,128)(2,1)S(1)}, bf16[128,512]{1,0:T(8,128)(2,1)S(1)}, u32[]{:S(2)}, u32[]{:S(2)}) %collective-permute-start) | collective-permute-done | bytes 131104 | tf_op jit(solution)/shard_map/ppermute | solution.py:443
  37.6 3.8 %collective-permute-done.1.refs_2_ = bf16[128,512]{1,0:T(8,128)(2,1)S(1)} collective-permute-done((bf16[128,512]{1,0:T(8,128)(2,1)S(1)}, bf16[128,512]{1,0:T(8,128)(2,1)S(1)}, u32[]{:S(2)}, u32[]{:S(2)}) %collective-permute-start.1) | collective-permute-done | bytes 131104 | tf_op jit(solution)/shard_map/ppermute | solution.py:443
  41.5 0.0 collective-permute-done.2.refs_3_
  41.5 2.4 %fine.1 = (bf16[128,512]{1,0:T(8,128)(2,1)S(1)}, bf16[128,512]{1,0:T(8,128)(2,1)S(1)}, bf16[128,512]{1,0:T(8,128)(2,1)S(1)}, bf16[128,512]{1,0:T(8,128)(2,1)S(1)}, f32[1,128]{1,0:T(1,128)S(1)}) custom-call(s32[1]{0:T(128)} %bitcast.place_ref, f32[96,512]{1,0:T(8,128)S(1)} %bitcast.19, f32[1,512]{1,0:T(1,128)S(1)} %bitcast.21, ...), custom_call_target="tpu_custom_call" | custom-call | flops 50331648 | bytes 2097152 | tf_op jit(solution)/shard_map/fine/pallas_call | solution.py:215
  43.9 0.7 copy-done.5
  44.6 0.0 all-to-all-done.got_ref
  44.6 0.4 coarse.1
  45.0 20.8 %all_to_all.10 = bf16[64,8,512]{2,1,0:T(8,128)(2,1)S(1)} all-to-all(bf16[64,8,512]{2,1,0:T(8,128)(2,1)S(1)} %coarse.1), channel_id=1, replica_groups=mesh['x'=4,'y'=4,'c'=2,'m'=4] {'x','y','m'}, dimensions={0} | all-to-all | bytes 1048576 | tf_op jit(solution)/shard_map/all_to_all | solution.py:467
  65.8 0.0 collective-permute-start.7
  65.8 1.0 %collective-permute-start.3 = (bf16[128,512]{1,0:T(8,128)(2,1)}, bf16[128,512]{1,0:T(8,128)(2,1)S(1)}, u32[]{:S(2)}, u32[]{:S(2)}) collective-permute-start(bf16[128,512]{1,0:T(8,128)(2,1)} %copy-done.5), channel_id=1, source_target_pairs={{0,3},{1,0},{2,1},{3,2},{4,7},{5,4},{6,5},{7,6},{8,11},{9,8},{10,9... | collective-permute-start | bytes 393224 | tf_op jit(solution)/shard_map/ppermute | solution.py:443
  66.8 1.7 %collective-permute-start.4 = (bf16[128,512]{1,0:T(8,128)(2,1)S(1)}, bf16[128,512]{1,0:T(8,128)(2,1)S(1)}, u32[]{:S(2)}, u32[]{:S(2)}) collective-permute-start(bf16[128,512]{1,0:T(8,128)(2,1)S(1)} %get-tuple-element.29), channel_id=1, source_target_pairs={{0,2},{1,3},{2,0},{3,1},{4,6},{5,7},{6,4},{7,5},{8,10},{9,11},{10,... | collective-permute-start | bytes 393224 | tf_op jit(solution)/shard_map/ppermute | solution.py:443
  68.5 0.1 collective-permute-start.5
  68.6 3.8 %collective-permute-done.3.refs_1_ = bf16[128,512]{1,0:T(8,128)(2,1)S(1)} collective-permute-done((bf16[128,512]{1,0:T(8,128)(2,1)}, bf16[128,512]{1,0:T(8,128)(2,1)S(1)}, u32[]{:S(2)}, u32[]{:S(2)}) %collective-permute-start.3) | collective-permute-done | bytes 131104 | tf_op jit(solution)/shard_map/ppermute | solution.py:443
  72.4 2.3 %collective-permute-done.4.refs_2_ = bf16[128,512]{1,0:T(8,128)(2,1)S(1)} collective-permute-done((bf16[128,512]{1,0:T(8,128)(2,1)S(1)}, bf16[128,512]{1,0:T(8,128)(2,1)S(1)}, u32[]{:S(2)}, u32[]{:S(2)}) %collective-permute-start.4) | collective-permute-done | bytes 131104 | tf_op jit(solution)/shard_map/ppermute | solution.py:443
  74.6 2.1 %collective-permute-done.5.refs_3_ = bf16[128,512]{1,0:T(8,128)(2,1)S(1)} collective-permute-done((bf16[128,512]{1,0:T(8,128)(2,1)S(1)}, bf16[128,512]{1,0:T(8,128)(2,1)S(1)}, u32[]{:S(2)}, u32[]{:S(2)}) %collective-permute-start.5) | collective-permute-done | bytes 131104 | tf_op jit(solution)/shard_map/ppermute | solution.py:443
  76.7 0.3 base.1
  77.0 0.4 near.1
  77.5 0.0 collective-permute-done.7.table_ref
  77.5 0.4 far.1
  77.9 8.8 %backward.1 = (bf16[2048,1024]{1,0:T(8,128)(2,1)}, f32[2]{0:T(128)}) custom-call(bf16[512,512]{1,0:T(8,128)(2,1)S(1)} %get-tuple-element.37.up_ref, bf16[2048,1024]{1,0:T(8,128)(2,1)} %get-tuple-element.38.slope_ref, bf16[96,1024]{1,0:T(8,128)(2,1)S(1)} %bitcast.27, bf16[1024,1024]{1,0:T(8,128)(2,1)S(1)} %copy-done.3, f32[1,128]{1,0:T(1,128)S(1)} %get-tuple-element.39.sums_ref), custom_call_target="tpu_custom_call" | custom-call | flops 4294967296 | bytes 16777216 | tf_op jit(solution)/shard_map/backward/pallas_call | solution.py:418
  (8 shorter events, 0.1 us)
Async XLA Ops:
  0.6 12.2 %copy-start.2 = (s32[512]{0:T(512)S(1)}, s32[512]{0:T(512)}, u32[]{:S(2)}) copy-start(s32[512]{0:T(512)} %param.15) | copy-start | bytes 6148
  0.6 40.9 %copy-start = (f32[512,96]{0,1:T(8,128)S(1)}, f32[512,96]{0,1:T(8,128)}, u32[]{:S(2)}) copy-start(f32[512,96]{0,1:T(8,128)} %param.13) | copy-start | bytes 589828
  0.7 40.8 %copy-start.1 = (f32[512]{0:T(512)S(1)}, f32[512]{0:T(512)}, u32[]{:S(2)}) copy-start(f32[512]{0:T(512)} %param.14) | copy-start | bytes 6148
  10.9 1.9 %collective-permute-start.6 = (bf16[512,512]{1,0:T(8,128)(2,1)S(1)}, bf16[512,512]{1,0:T(8,128)(2,1)S(1)}, u32[]{:S(2)}, u32[]{:S(2)}) collective-permute-start(bf16[512,512]{1,0:T(8,128)(2,1)S(1)} %get-tuple-element.22.pred_ref), channel_id=1, source_target_pairs={{0,4},{4,0},{1,5},{5,1},{2,6},{6,2},{3,7},{7,3},{8,12},{12,8},{9,1... | collective-permute-start | bytes 1572872 | tf_op jit(solution)/shard_map/ppermute | solution.py:459
  14.5 30.1 %all-to-all-start = ((bf16[64,8,512]{2,1,0:T(8,128)(2,1)}), bf16[64,8,512]{2,1,0:T(8,128)(2,1)S(1)}, u32[]{:S(2)}, u32[]{:S(2)}) async-start(bf16[64,8,512]{2,1,0:T(8,128)(2,1)} %bitcast.11), calls=%async_computation | async-start | bytes 1048576 | tf_op jit(solution)/shard_map/all_to_all | solution.py:463
  26.0 51.9 %copy-start.3 = (bf16[1024,1024]{1,0:T(8,128)(2,1)S(1)}, bf16[1024,1024]{1,0:T(8,128)(2,1)}, u32[]{:S(2)}) copy-start(bf16[1024,1024]{1,0:T(8,128)(2,1)} %w_ref.3) | copy-start | bytes 6291460
  26.0 51.9 %copy-start.4 = (bf16[1024,96]{0,1:T(8,128)(2,1)S(1)}, bf16[1024,96]{0,1:T(8,128)(2,1)}, u32[]{:S(2)}) copy-start(bf16[1024,96]{0,1:T(8,128)(2,1)} %param.11) | copy-start | bytes 589828
  26.1 11.6 %collective-permute-start = (bf16[128,512]{1,0:T(8,128)(2,1)S(1)}, bf16[128,512]{1,0:T(8,128)(2,1)S(1)}, u32[]{:S(2)}, u32[]{:S(2)}) collective-permute-start(bf16[128,512]{1,0:T(8,128)(2,1)S(1)} %get-tuple-element.24), channel_id=1, source_target_pairs={{0,1},{1,2},{2,3},{3,0},{4,5},{5,6},{6,7},{7,4},{8,9},{9,10},{10,1... | collective-permute-start | bytes 393224 | tf_op jit(solution)/shard_map/ppermute | solution.py:443
  27.7 13.8 %collective-permute-start.1 = (bf16[128,512]{1,0:T(8,128)(2,1)S(1)}, bf16[128,512]{1,0:T(8,128)(2,1)S(1)}, u32[]{:S(2)}, u32[]{:S(2)}) collective-permute-start(bf16[128,512]{1,0:T(8,128)(2,1)S(1)} %get-tuple-element.25), channel_id=1, source_target_pairs={{0,2},{1,3},{2,0},{3,1},{4,6},{5,7},{6,4},{7,5},{8,10},{9,11},{10,... | collective-permute-start | bytes 393224 | tf_op jit(solution)/shard_map/ppermute | solution.py:443
  30.4 11.1 %collective-permute-start.2 = (bf16[128,512]{1,0:T(8,128)(2,1)S(1)}, bf16[128,512]{1,0:T(8,128)(2,1)S(1)}, u32[]{:S(2)}, u32[]{:S(2)}) collective-permute-start(bf16[128,512]{1,0:T(8,128)(2,1)S(1)} %get-tuple-element.26), channel_id=1, source_target_pairs={{0,3},{1,0},{2,1},{3,2},{4,7},{5,4},{6,5},{7,6},{8,11},{9,8},{10,9... | collective-permute-start | bytes 393224 | tf_op jit(solution)/shard_map/ppermute | solution.py:443
  43.9 0.7 copy-start.5
  65.8 11.7 %collective-permute-start.7 = (bf16[512,512]{1,0:T(8,128)(2,1)S(1)}, bf16[512,512]{1,0:T(8,128)(2,1)S(1)}, u32[]{:S(2)}, u32[]{:S(2)}) collective-permute-start(bf16[512,512]{1,0:T(8,128)(2,1)S(1)} %bitcast.14), channel_id=1, source_target_pairs={{0,4},{4,0},{1,5},{5,1},{2,6},{6,2},{3,7},{7,3},{8,12},{12,8},{9,1... | collective-permute-start | bytes 1572872 | tf_op jit(solution)/shard_map/ppermute | solution.py:470
  65.8 6.6 %collective-permute-start.3 = (bf16[128,512]{1,0:T(8,128)(2,1)}, bf16[128,512]{1,0:T(8,128)(2,1)S(1)}, u32[]{:S(2)}, u32[]{:S(2)}) collective-permute-start(bf16[128,512]{1,0:T(8,128)(2,1)} %copy-done.5), channel_id=1, source_target_pairs={{0,3},{1,0},{2,1},{3,2},{4,7},{5,4},{6,5},{7,6},{8,11},{9,8},{10,9... | collective-permute-start | bytes 393224 | tf_op jit(solution)/shard_map/ppermute | solution.py:443
  66.8 7.9 %collective-permute-start.4 = (bf16[128,512]{1,0:T(8,128)(2,1)S(1)}, bf16[128,512]{1,0:T(8,128)(2,1)S(1)}, u32[]{:S(2)}, u32[]{:S(2)}) collective-permute-start(bf16[128,512]{1,0:T(8,128)(2,1)S(1)} %get-tuple-element.29), channel_id=1, source_target_pairs={{0,2},{1,3},{2,0},{3,1},{4,6},{5,7},{6,4},{7,5},{8,10},{9,11},{10,... | collective-permute-start | bytes 393224 | tf_op jit(solution)/shard_map/ppermute | solution.py:443
  68.5 8.2 %collective-permute-start.5 = (bf16[128,512]{1,0:T(8,128)(2,1)S(1)}, bf16[128,512]{1,0:T(8,128)(2,1)S(1)}, u32[]{:S(2)}, u32[]{:S(2)}) collective-permute-start(bf16[128,512]{1,0:T(8,128)(2,1)S(1)} %get-tuple-element.30), channel_id=1, source_target_pairs={{0,1},{1,2},{2,3},{3,0},{4,5},{5,6},{6,7},{7,4},{8,9},{9,10},{10,1... | collective-permute-start | bytes 393224 | tf_op jit(solution)/shard_map/ppermute | solution.py:443
